TPU v7x, 32 devices: a whole 2x2x4 slice. The times are simulated.
32 devices in a mesh: replica: 4 (over x, core), fsdp: 8 (over z, y).
Axes of the slice: x: 2, y: 2, z: 4, core: 2. Of those that a mesh axis runs over, the one named last changes fastest.
Arguments:
- tokens: bfloat16 [4096, 2048], P(('replica', 'fsdp')), may hold values from -6 to 6
- segments: int32 [4096], P(('replica', 'fsdp')), may hold values from 0 to 7, as said below
- cotangent: float32 [4096, 2048], P(('replica', 'fsdp')), may hold values from -6 to 6
- qkv_weight: bfloat16 [2048, 6144], P('fsdp'), may hold values from -1 to 1
- out_weight: bfloat16 [2048, 2048], P('fsdp'), may hold values from -0.125 to 0.125
- gate_up_weight: bfloat16 [2048, 16384], P('fsdp'), may hold values from -0.125 to 0.125
- down_weight: bfloat16 [8192, 2048], P('fsdp'), may hold values from -0.0625 to 0.0625
- q_gain: float32 [2048], replicated, may hold values from 0.5 to 5.5
- k_gain: float32 [2048], replicated, may hold values from 0.5 to 5.5
- attn_gain: float32 [2048], replicated, may hold values from 0.25 to 1.75
- mlp_gain: float32 [2048], replicated, may hold values from 0.25 to 1.75
Outputs:
- result: bfloat16 [4096, 2048], P(('replica', 'fsdp'))
- input_grad: float32 [4096, 2048], P(('replica', 'fsdp'))
- qkv_grad: float32 [2048, 6144], P('fsdp')
- out_grad: float32 [2048, 2048], P('fsdp')
- gate_up_grad: float32 [2048, 16384], P('fsdp')
- down_grad: float32 [8192, 2048], P('fsdp')
- q_gain_grad: float32 [2048], replicated
- k_gain_grad: float32 [2048], replicated
- attn_gain_grad: float32 [2048], replicated
- mlp_gain_grad: float32 [2048], replicated
Inputs may be any that keep to these rules, and one draw needn't show every extreme that they name: `segments`: within each sequence of 128 tokens, segment numbers start at 0 and rise by one at each cut; cuts fall only at multiples of 16 tokens, so each piece holds 16 to 128 tokens.
All inputs are finite; a program needn't handle non-finite values.
Results may differ from a plain program's by a relative error of at most 0.02.
The roundings to bfloat16 on the way count: a program that leaves them out, or rounds other values in their place, can miss the bound.
Values may be sent and summed in bfloat16 or wider, within the bound.
No kernel may reach another device: no remote copies, remote signals or barrier semaphores. Data moves between devices by JAX's collectives and lax.ppermute only.
A program may use at most 576 MiB of HBM per device.

v0:
```python
import jax
import jax.numpy as jnp
from jax import lax
from jax.experimental import pallas as pl
from jax.experimental.pallas import tpu as pltpu
from jax.sharding import PartitionSpec as P


D = 2048
HEADS = 16
HEAD_DIM = 128
FF = 8192
SEQ = 128


EPS = 1e-06
THETA = 500000.0
ROWS_DIMS = (((0,), (0,)), ((), ()))
COLS_DIMS = (((1,), (1,)), ((), ()))


def rms_scale(values):
    return lax.rsqrt(jnp.mean(values * values, axis=-1, keepdims=True) + EPS)


def rms_back(values, gain, upstream):
    factor = rms_scale(values)
    normed = values * factor
    d_normed = upstream * gain
    inner = jnp.mean(d_normed * normed, axis=-1, keepdims=True)
    return (factor * (d_normed - normed * inner), jnp.sum(upstream * normed, axis=0))


def rope_tables(count):
    half_dim = HEAD_DIM // 2
    freqs = THETA ** (-(2.0 * jnp.arange(half_dim).astype(jnp.float32)) / HEAD_DIM)
    places = (jnp.arange(count, dtype=jnp.int32) % SEQ).astype(jnp.float32)
    angles = places[:, None] * freqs[None, :]
    cosine = jnp.concatenate([jnp.cos(angles), jnp.cos(angles)], axis=1)[:, None, :]
    sine = jnp.concatenate([jnp.sin(angles), jnp.sin(angles)], axis=1)[:, None, :]
    return (cosine, sine)


def rotate(values, cosine, sine):
    half_dim = HEAD_DIM // 2
    turned = jnp.concatenate([-values[..., half_dim:], values[..., :half_dim]], axis=-1)
    return values * cosine + turned * sine


def rotate_back(upstream, cosine, sine):
    half_dim = HEAD_DIM // 2
    scaled = upstream * sine
    turned = jnp.concatenate([scaled[..., half_dim:], -scaled[..., :half_dim]], axis=-1)
    return upstream * cosine + turned


def masked_scores(queries, keys_b, seg_groups):
    scores = jnp.einsum("sqhd,skhd->shqk", queries, keys_b, preferred_element_type=jnp.float32)
    scores = scores * HEAD_DIM ** (-0.5)
    index = jnp.arange(SEQ, dtype=jnp.int32)
    causal = index[None, :] <= index[:, None]
    same = seg_groups[:, :, None] == seg_groups[:, None, :]
    allowed = (same & causal[None])[:, None]
    return jnp.where(allowed, scores, -1e30)


def fold_with(activations, incoming):
    return jnp.dot(activations, incoming, preferred_element_type=jnp.float32)


def back_with(upstream, incoming):
    return lax.dot_general(upstream, incoming, COLS_DIMS, preferred_element_type=jnp.float32)


def weight_grad(activations, upstream):
    return lax.psum_scatter(
        lax.dot_general(
            activations, upstream, ROWS_DIMS, preferred_element_type=jnp.float32
        ).astype(jnp.bfloat16),
        "fsdp",
        scatter_dimension=0,
        tiled=True,
    ).astype(jnp.float32)


def gathered(
    tokens,
    segments,
    cotangent,
    qkv_weight,
    out_weight,
    gate_up_weight,
    down_weight,
    q_gain,
    k_gain,
    attn_gain,
    mlp_gain,
):
    count = tokens.shape[0]
    groups = count // SEQ
    qkv = fold_with(tokens, lax.all_gather(qkv_weight, "fsdp", axis=0, tiled=True))
    q_pre, k_pre, v_pre = (qkv[:, :D], qkv[:, D : 2 * D], qkv[:, 2 * D :])
    q_norm = q_pre * rms_scale(q_pre) * q_gain
    k_norm = k_pre * rms_scale(k_pre) * k_gain
    cosine, sine = rope_tables(count)
    q_rot = rotate(q_norm.reshape(count, HEADS, HEAD_DIM), cosine, sine).astype(jnp.bfloat16)
    k_rot = rotate(k_norm.reshape(count, HEADS, HEAD_DIM), cosine, sine).astype(jnp.bfloat16)
    v_b = v_pre.astype(jnp.bfloat16)
    q_grp = q_rot.reshape(groups, SEQ, HEADS, HEAD_DIM)
    k_grp = k_rot.reshape(groups, SEQ, HEADS, HEAD_DIM)
    v_grp = v_b.reshape(groups, SEQ, HEADS, HEAD_DIM)
    seg_groups = segments.reshape(groups, SEQ)
    scores = masked_scores(q_grp, k_grp, seg_groups)
    top = jnp.max(scores, axis=-1, keepdims=True)
    lse = top + jnp.log(jnp.sum(jnp.exp(scores - top), axis=-1, keepdims=True))
    prob_b = jnp.exp(scores - lse).astype(jnp.bfloat16)
    attn = jnp.einsum("shqk,skhd->sqhd", prob_b, v_grp, preferred_element_type=jnp.float32)
    attn_b = attn.reshape(count, D).astype(jnp.bfloat16)
    pre_attn = fold_with(attn_b, lax.all_gather(out_weight, "fsdp", axis=0, tiled=True))
    mid = tokens.astype(jnp.float32) + pre_attn * rms_scale(pre_attn) * attn_gain
    mid_b = mid.astype(jnp.bfloat16)
    gate_up = fold_with(mid_b, lax.all_gather(gate_up_weight, "fsdp", axis=0, tiled=True))
    gate, upper = (gate_up[:, :FF], gate_up[:, FF:])
    sigma = jax.nn.sigmoid(gate)
    hidden_b = (gate * sigma * upper).astype(jnp.bfloat16)
    pre_mlp = fold_with(hidden_b, lax.all_gather(down_weight, "fsdp", axis=0, tiled=True))
    result = (mid + pre_mlp * rms_scale(pre_mlp) * mlp_gain).astype(jnp.bfloat16)
    d_pre_mlp, mlp_gain_part = rms_back(pre_mlp, mlp_gain, cotangent)
    dmlp_b = d_pre_mlp.astype(jnp.bfloat16)
    down_part = weight_grad(hidden_b, dmlp_b)
    d_hidden = back_with(dmlp_b, lax.all_gather(down_weight, "fsdp", axis=0, tiled=True))
    d_gate = d_hidden * upper * sigma * (1.0 + gate * (1.0 - sigma))
    d_upper = d_hidden * gate * sigma
    dgu_b = jnp.concatenate([d_gate, d_upper], axis=1).astype(jnp.bfloat16)
    gate_up_part = weight_grad(mid_b, dgu_b)
    d_mid = cotangent + back_with(dgu_b, lax.all_gather(gate_up_weight, "fsdp", axis=0, tiled=True))
    d_pre_attn, attn_gain_part = rms_back(pre_attn, attn_gain, d_mid)
    dattn_in_b = d_pre_attn.astype(jnp.bfloat16)
    out_part = weight_grad(attn_b, dattn_in_b)
    d_attn_b = back_with(dattn_in_b, lax.all_gather(out_weight, "fsdp", axis=0, tiled=True)).astype(
        jnp.bfloat16
    )
    d_attn_grp = d_attn_b.reshape(groups, SEQ, HEADS, HEAD_DIM)
    prob = jnp.exp(masked_scores(q_grp, k_grp, seg_groups) - lse)
    d_value = jnp.einsum("shqk,sqhd->skhd", prob_b, d_attn_grp, preferred_element_type=jnp.float32)
    d_prob = jnp.einsum("sqhd,skhd->shqk", d_attn_grp, v_grp, preferred_element_type=jnp.float32)
    delta = jnp.sum(prob * d_prob, axis=-1, keepdims=True)
    ds_b = (prob * (d_prob - delta) * HEAD_DIM ** (-0.5)).astype(jnp.bfloat16)
    dq_rot = jnp.einsum("shqk,skhd->sqhd", ds_b, k_grp, preferred_element_type=jnp.float32)
    dk_rot = jnp.einsum("shqk,sqhd->skhd", ds_b, q_grp, preferred_element_type=jnp.float32)
    d_q_norm = rotate_back(dq_rot.reshape(count, HEADS, HEAD_DIM), cosine, sine).reshape(count, D)
    d_k_norm = rotate_back(dk_rot.reshape(count, HEADS, HEAD_DIM), cosine, sine).reshape(count, D)
    d_q_pre, q_gain_part = rms_back(q_pre, q_gain, d_q_norm)
    d_k_pre, k_gain_part = rms_back(k_pre, k_gain, d_k_norm)
    dqkv_b = jnp.concatenate([d_q_pre, d_k_pre, d_value.reshape(count, D)], axis=1).astype(
        jnp.bfloat16
    )
    qkv_part = weight_grad(tokens, dqkv_b)
    input_grad = d_mid + back_with(dqkv_b, lax.all_gather(qkv_weight, "fsdp", axis=0, tiled=True))
    qkv_grad, out_grad, gate_up_grad, down_grad = (
        lax.psum(qkv_part.astype(jnp.bfloat16), "replica").astype(jnp.float32),
        lax.psum(out_part.astype(jnp.bfloat16), "replica").astype(jnp.float32),
        lax.psum(gate_up_part.astype(jnp.bfloat16), "replica").astype(jnp.float32),
        lax.psum(down_part.astype(jnp.bfloat16), "replica").astype(jnp.float32),
    )
    q_gain_grad, k_gain_grad, attn_gain_grad, mlp_gain_grad = lax.psum(
        (q_gain_part, k_gain_part, attn_gain_part, mlp_gain_part), ("replica", "fsdp")
    )
    return (
        result,
        input_grad,
        qkv_grad,
        out_grad,
        gate_up_grad,
        down_grad,
        q_gain_grad,
        k_gain_grad,
        attn_gain_grad,
        mlp_gain_grad,
    )


def swap_pairs(count, bits):
    return [(i, i ^ bits) for i in range(count)]


def lane_pairs(hops):
    return [(2 * a + y, 2 * b + y) for a, b in hops for y in range(2)]


OUTER_IN = ((3, 2), (0, 1))
INNER_OUT = ((2, 3), (1, 0))
MIDDLE = ((1, 2), (2, 1))


def hop(value, bits):
    return lax.ppermute(value, "fsdp", swap_pairs(8, bits))


def lane(value, hops):
    return lax.ppermute(value, "fsdp", lane_pairs(hops))


BF16 = jnp.bfloat16
F32 = jnp.float32


def spread(own, early=None, late=None):
    s1 = hop(own, 1)
    s2 = hop(own, 2)
    near = lane(own, MIDDLE)
    if early is not None:
        s2, near = early(s2, near)
    s3 = hop(s2, 1)
    far = lane(s2, MIDDLE)
    if late is not None:
        far = late(far)
    s4 = far + lane(near, INNER_OUT)
    s5 = hop(s4, 1)
    s6 = near + lane(far, INNER_OUT)
    s7 = hop(s6, 1)
    return [own, s1, s2, s3, s4, s5, s6, s7]


def collect(make):
    narrow = lambda value: value.astype(jnp.bfloat16)
    wide = lambda value: value.astype(jnp.float32)
    held = {}
    for j in (3, 2, 1, 0):
        part = make(j)
        held[j] = part[0] + wide(hop(narrow(part[1]), 1))
    far = held[2] + wide(lane(narrow(held[3]), OUTER_IN))
    near = held[3] + wide(lane(narrow(held[2]), OUTER_IN))
    next_to = held[1] + wide(lane(narrow(far), MIDDLE))
    near_got = wide(lane(narrow(near), MIDDLE))
    return held[0] + near_got + wide(hop(narrow(next_to), 2))


def core_hop(value):
    return lax.ppermute(value, "replica", swap_pairs(4, 1))


def chip_hop(value):
    return lax.ppermute(value, "replica", swap_pairs(4, 2))


def absolute(blocks, index):
    held = jnp.zeros((len(blocks),) + blocks[0].shape, blocks[0].dtype)
    for k, block in enumerate(blocks):
        held = lax.dynamic_update_slice_in_dim(held, block[None], index ^ k, axis=0)
    return held


def swap_blocks(block_for):
    return [block_for(0)] + [hop(block_for(k), k) for k in range(1, 8)]


def replica_gather(block):
    across = chip_hop(block)
    return [block, core_hop(block), across, core_hop(across)]


def call(body, grid, ins, outs, shapes, flops=0, moved=0, scalars=0):
    return pl.pallas_call(
        body,
        grid_spec=pltpu.PrefetchScalarGridSpec(
            num_scalar_prefetch=scalars, grid=grid, in_specs=ins, out_specs=outs
        ),
        out_shape=shapes,
        compiler_params=pltpu.CompilerParams(
            dimension_semantics=("arbitrary",) * len(grid), vmem_limit_bytes=32 * 1024 * 1024
        ),
        cost_estimate=pl.CostEstimate(flops=flops, bytes_accessed=moved, transcendentals=0),
    )


def pair_body(own, got, out):
    for k in range(8):
        out[k] = own[k] + got[k ^ 1]


def sum_body(inverse, *refs):
    out = refs[-1]
    for k in range(8):
        total = refs[0][k]
        for j in range(1, 4):
            total = total + refs[j][k ^ (2 * j)]
        out[k] = total
        out[k, :2] = lax.rsqrt(total[:2] / D + EPS) if inverse else total[:2] / D


def slot_mean(values, inverse):
    spec = pl.BlockSpec(values.shape, lambda i: (0, 0, 0))
    shape = jax.ShapeDtypeStruct(values.shape, F32)
    pair = call(pair_body, (1,), [spec] * 2, spec, shape)(values, hop(values, 1))
    parts = [pair] + [hop(pair, bits) for bits in (2, 4, 6)]
    return call(lambda *refs: sum_body(inverse, *refs), (1,), [spec] * 4, spec, shape)(*parts)


def diagonal():
    down = lax.broadcasted_iota(jnp.int32, (SEQ, SEQ), 0)
    right = lax.broadcasted_iota(jnp.int32, (SEQ, SEQ), 1)
    return down, right


def upright(row):
    down, right = diagonal()
    return jnp.sum(jnp.where(down == right, row, 0.0), axis=1, keepdims=True)


def flat(column):
    down, right = diagonal()
    return jnp.sum(jnp.where(down == right, column, 0.0), axis=0, keepdims=True)


def nt(a, b):
    return lax.dot_general(a, b, COLS_DIMS, preferred_element_type=F32)


def tn(a, b):
    return lax.dot_general(a, b, ROWS_DIMS, preferred_element_type=F32)


def allowed_pairs(fac_ref):
    down, right = diagonal()
    row = fac_ref[0, 2:3, :]
    return (upright(row) == row) & (right <= down)


def softmax(q, k, allowed):
    scores = jnp.where(allowed, nt(q, k) * HEAD_DIM ** (-0.5), -1e30)
    top = jnp.max(scores, axis=1, keepdims=True)
    lse = top + jnp.log(jnp.sum(jnp.exp(scores - top), axis=1, keepdims=True))
    return jnp.exp(scores - lse)


def attend_body(qkv_ref, fac_ref, gain_ref, cos_ref, sin_ref, rot_ref, attn_ref):
    for n in range(fac_ref.shape[0]):
        at = pl.ds(n * SEQ, SEQ)
        one = pl.ds(n, 1)
        attend_one(
            qkv_ref.at[at], fac_ref.at[one], gain_ref, cos_ref, sin_ref, rot_ref.at[at], attn_ref.at[at]
        )


def attend_one(qkv_ref, fac_ref, gain_ref, cos_ref, sin_ref, rot_ref, attn_ref):
    wide = attn_ref.shape[1]
    allowed = allowed_pairs(fac_ref)
    cosine, sine = cos_ref[...], sin_ref[...]
    factor = [upright(fac_ref[0, i : i + 1, :]) for i in range(2)]
    for h in range(wide // HEAD_DIM):
        turned = []
        for i in range(2):
            at = slice(i * wide + h * HEAD_DIM, i * wide + (h + 1) * HEAD_DIM)
            value = qkv_ref[:, at] * factor[i] * gain_ref[i : i + 1, h * HEAD_DIM : (h + 1) * HEAD_DIM]
            value = value * cosine + pltpu.roll(value, HEAD_DIM // 2, 1) * sine
            turned.append(value.astype(BF16))
            rot_ref[:, at] = turned[i]
        at = slice(2 * wide + h * HEAD_DIM, 2 * wide + (h + 1) * HEAD_DIM)
        value_b = qkv_ref[:, at].astype(BF16)
        rot_ref[:, at] = value_b
        prob_b = softmax(turned[0], turned[1], allowed).astype(BF16)
        attn = jnp.dot(prob_b, value_b, preferred_element_type=F32)
        attn_ref[:, h * HEAD_DIM : (h + 1) * HEAD_DIM] = attn.astype(BF16)


def attend_back_body(
    rot_ref, up_ref, qkv_ref, fac_ref, gain_ref, cos_ref, sin_ref, dn_ref, dv_ref, inner_ref, sum_ref
):
    @pl.when(pl.program_id(0) == 0)
    def _():
        sum_ref[...] = jnp.zeros_like(sum_ref)

    for n in range(fac_ref.shape[0]):
        at = pl.ds(n * SEQ, SEQ)
        one = pl.ds(n, 1)
        attend_back_one(
            rot_ref.at[at],
            up_ref.at[at],
            qkv_ref.at[at],
            fac_ref.at[one],
            gain_ref,
            cos_ref,
            sin_ref,
            dn_ref.at[at],
            dv_ref.at[at],
            inner_ref.at[one],
            sum_ref,
        )


def attend_back_one(
    rot_ref, up_ref, qkv_ref, fac_ref, gain_ref, cos_ref, sin_ref, dn_ref, dv_ref, inner_ref, sum_ref
):
    wide = up_ref.shape[1]
    allowed = allowed_pairs(fac_ref)
    cosine, sine = cos_ref[...], sin_ref[...]
    factor = [upright(fac_ref[0, i : i + 1, :]) for i in range(2)]
    inner = [0.0, 0.0]
    for h in range(wide // HEAD_DIM):
        own = slice(h * HEAD_DIM, (h + 1) * HEAD_DIM)
        q, k, v = (
            rot_ref[:, i * wide + h * HEAD_DIM : i * wide + (h + 1) * HEAD_DIM] for i in range(3)
        )
        up = up_ref[:, own]
        prob = softmax(q, k, allowed)
        dv_ref[:, own] = tn(prob.astype(BF16), up).astype(BF16)
        d_prob = nt(up, v)
        delta = jnp.sum(prob * d_prob, axis=1, keepdims=True)
        ds_b = (prob * (d_prob - delta) * HEAD_DIM ** (-0.5)).astype(BF16)
        back = (jnp.dot(ds_b, k, preferred_element_type=F32), tn(ds_b, q))
        for i in range(2):
            at = slice(i * wide + h * HEAD_DIM, i * wide + (h + 1) * HEAD_DIM)
            d_norm = back[i] * cosine + pltpu.roll(back[i] * sine, HEAD_DIM // 2, 1)
            dn_ref[:, at] = d_norm
            unit = qkv_ref[:, at] * factor[i]
            inner[i] = inner[i] + jnp.sum(
                d_norm * gain_ref[i : i + 1, own] * unit, axis=1, keepdims=True
            )
            sum_ref[i : i + 1, own] += jnp.sum(d_norm * unit, axis=0, keepdims=True)
    for i in range(2):
        inner_ref[0, i : i + 1, :] = flat(inner[i])


def norm_back_body(dn_ref, dv_ref, qkv_ref, fac_ref, mean_ref, gain_ref, out_ref):
    wide = dv_ref.shape[1]
    for i in range(2):
        at = slice(i * wide, (i + 1) * wide)
        factor = upright(fac_ref[0, i : i + 1, :])
        mean = upright(mean_ref[0, i : i + 1, :])
        unit = qkv_ref[:, at] * factor
        value = factor * (dn_ref[:, at] * gain_ref[i : i + 1, :] - unit * mean)
        out_ref[:, at] = value.astype(BF16)
    out_ref[:, 2 * wide :] = dv_ref[...]


def gate_up_body(copy_ref, *refs):
    out = refs[-1]
    width = refs[0].shape[2]
    for m in range(4):
        start = pl.multiple_of((copy_ref[0] ^ m) * width, width)
        out[:, pl.ds(start, width)] = refs[m][0].astype(F32)


def qkv_body(copy_ref, *refs):
    out = refs[-1]
    members, height, width = refs[0].shape
    for m in range(4):
        start = pl.multiple_of((copy_ref[0] ^ m) * height, height)
        for i in range(members):
            out[pl.ds(start, height), i * width : (i + 1) * width] = refs[m][i].astype(F32)


def halves(left, right, core, height):
    own = lax.dynamic_slice_in_dim(left, core * height, height, axis=1)
    other = lax.dynamic_slice_in_dim(left, (1 - core) * height, height, axis=1)
    return (tn(own, right) + core_hop(tn(other, right).astype(BF16)).astype(F32)).astype(BF16)


def join_halves(pair_b, other, core):
    total = (pair_b.astype(F32) + other.astype(F32)).astype(BF16)
    back = core_hop(total)
    first = jnp.where(core == 0, total, back)
    second = jnp.where(core == 0, back, total)
    return jnp.concatenate([first, second]).astype(F32)


tie = lax.optimization_barrier


def tensor_split(
    tokens,
    segments,
    cotangent,
    qkv_weight,
    out_weight,
    gate_up_weight,
    down_weight,
    q_gain,
    k_gain,
    attn_gain,
    mlp_gain,
):
    members, copies = 8, 4
    rows = tokens.shape[0]
    count = members * rows
    wide = D // members
    units = FF // members
    quarter = units // copies
    place = lax.axis_index("fsdp")
    copy = lax.axis_index("replica")
    core = copy % 2
    owned = qkv_weight.shape[0]
    sub = owned // copies
    copy_at = copy.astype(jnp.int32).reshape(1)

    def qkv_block(k):
        parts = [
            lax.dynamic_slice(qkv_weight, (copy * sub, i * D + (place ^ k) * wide), (sub, wide))
            for i in range(3)
        ]
        return jnp.concatenate(parts, axis=1)

    def gate_up_block(member):
        parts = [
            lax.dynamic_slice_in_dim(
                gate_up_source, i * FF + member * units + copy * quarter, quarter, axis=1
            )
            for i in range(2)
        ]
        return jnp.concatenate(parts, axis=1)

    mine = lambda gain: lax.dynamic_slice_in_dim(gain, place * wide, wide)
    gain_own = jnp.stack([mine(q_gain), mine(k_gain)])

    qkv_blocks = swap_blocks(qkv_block)
    gate_up_source = gate_up_weight

    def early(s2, near):
        nonlocal gate_up_source
        s2, near, gate_up_source = tie((s2, near, gate_up_weight))
        return s2, near

    def late(far):
        nonlocal qkv_blocks
        far, qkv_blocks = tie((far, qkv_blocks))
        return far

    token_slots = spread(tokens, early, late)
    pieces = absolute(replica_gather(absolute(qkv_blocks, place)), copy)
    qkv_cols = pieces.transpose(1, 0, 2, 3).reshape(D, 3 * wide)
    cosine, sine = rope_tables(rows)
    sign = jnp.where(jnp.arange(HEAD_DIM) < HEAD_DIM // 2, -1.0, 1.0)
    cosine, sine = cosine[:, 0], sine[:, 0] * sign

    token_all = jnp.concatenate(token_slots)
    qkv = fold_with(token_all, qkv_cols)
    gate_up_piece = jnp.stack([gate_up_block(i) for i in range(members)])
    gate_up_piece = lax.all_to_all(gate_up_piece, "fsdp", 0, 0, tiled=True).reshape(D, 2 * quarter)

    q_pre, k_pre = (qkv[:, :wide], qkv[:, wide : 2 * wide])
    squares = [jnp.sum(value * value, axis=1).reshape(members, rows) for value in (q_pre, k_pre)]
    seg_rows = jnp.zeros((members, rows), F32).at[0].set(segments.astype(F32))
    factors = slot_mean(jnp.stack(squares + [seg_rows], axis=1), True)
    slab = lambda width, n=1: pl.BlockSpec((n * rows, width), lambda i: (i, 0))
    line = lambda height, n=1: pl.BlockSpec((n, height, rows), lambda i: (i, 0, 0))
    whole = lambda shape: pl.BlockSpec(shape, lambda i: (0,) * len(shape))
    tables = [whole((2, wide)), whole((rows, HEAD_DIM)), whole((rows, HEAD_DIM))]
    rot, attn_b = call(
        attend_body,
        (members // 2,),
        [slab(3 * wide, 2), line(3, 2)] + tables,
        [slab(3 * wide, 2), slab(wide, 2)],
        [jax.ShapeDtypeStruct((count, 3 * wide), BF16), jax.ShapeDtypeStruct((count, wide), BF16)],
        flops=4 * count * rows * wide,
        moved=count * wide * 20,
    )(qkv, factors, gain_own, cosine, sine)

    span = 2 * rows
    rows_of = lambda value, j: value[j * span : (j + 1) * span]
    pre_attn = collect(lambda j: fold_with(rows_of(attn_b, j), out_weight).reshape(2, rows, D))
    gate_up_all = replica_gather(gate_up_piece)
    mid = tokens.astype(F32) + pre_attn * rms_scale(pre_attn) * attn_gain
    mid_b = mid.astype(BF16)

    def late_mid(far):
        nonlocal gate_up_all
        far, gate_up_all = tie((far, gate_up_all))
        return far

    mid_all = jnp.concatenate(spread(mid_b, None, late_mid))
    gate_up_cols = absolute(gate_up_all, copy)
    gate_up = [fold_with(mid_all, gate_up_cols[c]) for c in range(copies)]
    gate = [value[:, :quarter] for value in gate_up]
    upper = [value[:, quarter:] for value in gate_up]
    sigma = [jax.nn.sigmoid(value) for value in gate]
    hidden_b = jnp.concatenate(
        [(g * s * u).astype(BF16) for g, s, u in zip(gate, sigma, upper)], axis=1
    )
    pre_mlp = collect(lambda j: fold_with(rows_of(hidden_b, j), down_weight).reshape(2, rows, D))
    result = (mid + pre_mlp * rms_scale(pre_mlp) * mlp_gain).astype(BF16)
    d_pre_mlp, mlp_gain_part = rms_back(pre_mlp, mlp_gain, cotangent)
    dmlp_b = d_pre_mlp.astype(BF16)

    dmlp_all = jnp.concatenate(spread(dmlp_b))
    d_hidden = back_with(dmlp_all, down_weight)
    dgu = []
    for c in range(copies):
        d_h = d_hidden[:, c * quarter : (c + 1) * quarter]
        d_gate = d_h * upper[c] * sigma[c] * (1.0 + gate[c] * (1.0 - sigma[c]))
        d_upper = d_h * gate[c] * sigma[c]
        dgu.append(jnp.concatenate([d_gate, d_upper], axis=1).astype(BF16))

    def d_mid_part(j):
        total = back_with(rows_of(dgu[0], j), gate_up_cols[0])
        for c in range(1, copies):
            total = total + back_with(rows_of(dgu[c], j), gate_up_cols[c])
        return total.reshape(2, rows, D)

    dgu_all = jnp.stack(dgu)
    quarter_grad = lambda m: tn(
        mid_all, lax.dynamic_index_in_dim(dgu_all, copy ^ m, axis=0, keepdims=False)
    )
    kept = {}

    def d_mid_step(j):
        if j == 1:
            pair = halves(hidden_b, dmlp_all, core, units // 2)
            dgu[0], kept["pair"] = tie((dgu[0], pair))
            kept["down"] = chip_hop(kept["pair"])
        if j == 0:
            sends = [quarter_grad(m).astype(BF16) for m in (3, 1)]
            dgu[0], *sends = tie((dgu[0], *sends))
            kept[3], kept[1] = (core_hop(value) for value in sends)
            sent = (quarter_grad(2) + kept[3].astype(F32)).astype(BF16)
            kept[2] = chip_hop(sent)
            kept[0] = quarter_grad(0) + kept[1].astype(F32)
        return d_mid_part(j)

    d_mid = cotangent + collect(d_mid_step)
    d_mid, gate_up_own = tie((d_mid, kept[0]))
    down_pair, down_other = kept["pair"], kept["down"]
    gate_up_part = (gate_up_own + kept[2].astype(F32)).astype(BF16)

    d_pre_attn, attn_gain_part = rms_back(pre_attn, attn_gain, d_mid)
    dattn_all = jnp.concatenate(spread(d_pre_attn.astype(BF16)))
    dattn_all, gate_up_part = tie((dattn_all, gate_up_part))
    d_attn_b = back_with(dattn_all, out_weight).astype(BF16)
    gate_up_part = gate_up_part.reshape(members, owned, 2 * quarter)
    gate_up_part = lax.all_to_all(gate_up_part, "fsdp", 0, 0, tiled=True)
    attend_back = call(
        attend_back_body,
        (members // 2,),
        [slab(3 * wide, 2), slab(wide, 2), slab(3 * wide, 2), line(3, 2)] + tables,
        [slab(2 * wide, 2), slab(wide, 2), line(2, 2), whole((2, wide))],
        [
            jax.ShapeDtypeStruct((count, 2 * wide), F32),
            jax.ShapeDtypeStruct((count, wide), BF16),
            jax.ShapeDtypeStruct((members, 2, rows), F32),
            jax.ShapeDtypeStruct((2, wide), F32),
        ],
        flops=10 * count * rows * wide,
        moved=count * wide * 30,
    )
    d_norm, d_value, inner, gain_sums = attend_back(rot, d_attn_b, qkv, factors, gain_own, cosine, sine)
    inner, dattn_late = tie((inner, dattn_all))
    means = slot_mean(inner, False)
    means, down_pair = tie((means, down_pair))
    out_pair = halves(attn_b, dattn_late, core, wide // 2)
    out_other = chip_hop(out_pair)
    dqkv_b = call(
        norm_back_body,
        (members,),
        [slab(2 * wide), slab(wide), slab(3 * wide), line(3), line(2), whole((2, wide))],
        slab(3 * wide),
        jax.ShapeDtypeStruct((count, 3 * wide), BF16),
        flops=count * wide * 10,
        moved=count * wide * 28,
    )(d_norm, d_value, qkv, factors, means, gain_own)
    blank = jnp.zeros((2, D), F32)
    gains = jnp.concatenate(
        [
            lax.dynamic_update_slice_in_dim(blank, gain_sums, place * wide, axis=1),
            attn_gain_part[None],
            mlp_gain_part[None],
        ]
    )
    gains = gains + chip_hop(gains)
    gains = gains + core_hop(gains)
    for bits in (1, 2, 4):
        gains = gains + hop(gains, bits)
    down_grad = join_halves(down_pair, down_other, core)
    dqkv_b, out_other = tie((dqkv_b, out_other))

    qkv_full = tn(token_all, dqkv_b).reshape(members, copies, sub, 3 * wide)
    part_for = lambda m: lax.dynamic_index_in_dim(qkv_full, copy ^ m, axis=1, keepdims=False)
    third, first = part_for(3).astype(BF16), part_for(1).astype(BF16)
    dqkv_b, third, first = tie((dqkv_b, third, first))
    qkv_sent = (part_for(2) + core_hop(third).astype(F32)).astype(BF16)
    qkv_own = part_for(0) + core_hop(first).astype(F32)
    qkv_part = (qkv_own + chip_hop(qkv_sent).astype(F32)).astype(BF16)
    gate_up_parts = replica_gather(gate_up_part)
    qkv_blocks = swap_blocks(
        lambda k: lax.dynamic_index_in_dim(qkv_part, place ^ k, axis=0, keepdims=False)
    )
    input_grad = d_mid + collect(
        lambda j: back_with(rows_of(dqkv_b, j), qkv_cols).reshape(2, rows, D)
    )
    out_grad = join_halves(out_pair, out_other, core)
    gate_up_grad = call(
        gate_up_body,
        (2, members),
        [pl.BlockSpec((1, owned, quarter), lambda h, i, c: (i, 0, h))] * copies,
        pl.BlockSpec((owned, units), lambda h, i, c: (0, h * members + i)),
        jax.ShapeDtypeStruct((owned, 2 * FF), F32),
        moved=owned * FF * 12,
        scalars=1,
    )(copy_at, *gate_up_parts)
    qkv_blocks, out_grad, gains = tie((qkv_blocks, out_grad, gains))
    qkv_grad = call(
        qkv_body,
        (3,),
        [pl.BlockSpec((members, sub, wide), lambda i, c: (0, 0, i))] * copies,
        pl.BlockSpec((owned, D), lambda i, c: (0, i)),
        jax.ShapeDtypeStruct((owned, 3 * D), F32),
        moved=owned * D * 18,
        scalars=1,
    )(copy_at, *replica_gather(absolute(qkv_blocks, place)))
    return (
        result,
        input_grad,
        qkv_grad,
        out_grad,
        gate_up_grad,
        down_grad,
        gains[0],
        gains[1],
        gains[2],
        gains[3],
    )


def solution(mesh):
    def per_device(*arrays):
        fits = mesh.shape["fsdp"] == 8 and mesh.shape["replica"] == 4 and arrays[0].shape[0] == SEQ
        if not fits:
            return gathered(*arrays)
        return tensor_split(*arrays)


    placed = (
        P(("replica", "fsdp"), None),
        P(("replica", "fsdp")),
        P(("replica", "fsdp"), None),
        P("fsdp", None),
        P("fsdp", None),
        P("fsdp", None),
        P("fsdp", None),
        P(),
        P(),
        P(),
        P(),
    )
    return jax.shard_map(
        per_device,
        mesh=mesh,
        in_specs=placed,
        out_specs=(
            P(("replica", "fsdp"), None),
            P(("replica", "fsdp"), None),
            P("fsdp", None),
            P("fsdp", None),
            P("fsdp", None),
            P("fsdp", None),
            P(),
            P(),
            P(),
            P(),
        ),
        check_vma=False,
    )
```

profile of v0, /device:TPU:0, one launch (start us, length us, event | category | flops | bytes accessed | tf_op | source)
XLA Modules:
  0.0 822.7 jit_solution(14151081238932388660)
XLA Ops:
  47.5 6.4 collective-permute-done.3
  54.7 7.6 collective-permute-done.12
  68.5 5.7 all-to-all-start
  74.7 5.4 collective-permute-done.13
  80.2 12.0 %collective-permute-done.14 = bf16[128,2048]{1,0:T(8,128)(2,1)} collective-permute-done((bf16[128,2048]{1,0:T(8,128)(2,1)}, bf16[128,2048]{1,0:T(8,128)(2,1)}, u32[]{:S(2)}, u32[]{:S(2)}) %collective-permute-start.14) | collective-permute-done | bytes 524320 | tf_op jit(solution)/shard_map/ppermute | solution.py:201
  93.3 6.9 collective-permute-start.15
  100.3 12.2 %collective-permute-done.15 = bf16[128,2048]{1,0:T(8,128)(2,1)S(1)} collective-permute-done((bf16[128,2048]{1,0:T(8,128)(2,1)S(1)}, bf16[128,2048]{1,0:T(8,128)(2,1)S(1)}, u32[]{:S(2)}, u32[]{:S(2)}) %collective-permute-start.15) | collective-permute-done | bytes 524320 | tf_op jit(solution)/shard_map/ppermute | solution.py:197
  130.4 6.8 shard_map.188
  140.4 6.6 collective-permute-done.25
  152.6 7.1 collective-permute-done.26
  161.0 5.3 collective-permute-start.29
  177.9 9.6 %collective-permute-start.31 = (bf16[128,2048]{1,0:T(8,128)(2,1)S(1)}, bf16[128,2048]{1,0:T(8,128)(2,1)S(1)}, u32[]{:S(2)}, u32[]{:S(2)}) collective-permute-start(bf16[128,2048]{1,0:T(8,128)(2,1)S(1)} %fusion.27), channel_id=1, source_target_pairs={{0,2},{1,3},{2,0},{3,1},{4,6},{5,7},{6,4},{7,5},{8,10},{9,11},{10,... | collective-permute-start | bytes 1572872 | tf_op jit(solution)/shard_map/ppermute | solution.py:197
  187.5 9.3 %collective-permute-done.37 = bf16[2048,512]{1,0:T(8,128)(2,1)S(1)} collective-permute-done((bf16[2048,512]{1,0:T(8,128)(2,1)}, bf16[2048,512]{1,0:T(8,128)(2,1)S(1)}, u32[]{:S(2)}, u32[]{:S(2)}) %collective-permute-start.37) | collective-permute-done | bytes 2097184 | tf_op jit(solution)/shard_map/ppermute | solution.py:244
  199.7 12.2 %collective-permute-done.33 = bf16[128,2048]{1,0:T(8,128)(2,1)S(1)} collective-permute-done((bf16[128,2048]{1,0:T(8,128)(2,1)S(1)}, bf16[128,2048]{1,0:T(8,128)(2,1)S(1)}, u32[]{:S(2)}, u32[]{:S(2)}) %collective-permute-start.33) | collective-permute-done | bytes 524320 | tf_op jit(solution)/shard_map/ppermute | solution.py:197
  215.3 10.0 %collective-permute-done.34 = bf16[128,2048]{1,0:T(8,128)(2,1)S(1)} collective-permute-done((bf16[128,2048]{1,0:T(8,128)(2,1)S(1)}, bf16[128,2048]{1,0:T(8,128)(2,1)S(1)}, u32[]{:S(2)}, u32[]{:S(2)}) %collective-permute-start.34) | collective-permute-done | bytes 524320 | tf_op jit(solution)/shard_map/ppermute | solution.py:197
  226.7 4.7 collective-permute-done.40
  238.4 7.5 collective-permute-done.41
  248.1 9.4 %collective-permute-done.43 = bf16[128,2048]{1,0:T(8,128)(2,1)S(1)} collective-permute-done((bf16[128,2048]{1,0:T(8,128)(2,1)S(1)}, bf16[128,2048]{1,0:T(8,128)(2,1)S(1)}, u32[]{:S(2)}, u32[]{:S(2)}) %collective-permute-start.43) | collective-permute-done | bytes 524320 | tf_op jit(solution)/shard_map/ppermute | solution.py:197
  275.7 11.4 %collective-permute-done.46 = bf16[128,2048]{1,0:T(8,128)(2,1)S(1)} collective-permute-done((bf16[128,2048]{1,0:T(8,128)(2,1)S(1)}, bf16[128,2048]{1,0:T(8,128)(2,1)S(1)}, u32[]{:S(2)}, u32[]{:S(2)}) %collective-permute-start.46) | collective-permute-done | bytes 524320 | tf_op jit(solution)/shard_map/ppermute | solution.py:197
  294.0 5.7 collective-permute-done.47
  300.0 4.4 collective-permute-start.50
  318.7 8.1 collective-permute-start.52
  326.7 10.0 %collective-permute-done.52 = bf16[128,2048]{1,0:T(8,128)(2,1)S(1)} collective-permute-done((bf16[128,2048]{1,0:T(8,128)(2,1)S(1)}, bf16[128,2048]{1,0:T(8,128)(2,1)S(1)}, u32[]{:S(2)}, u32[]{:S(2)}) %collective-permute-start.52) | collective-permute-done | bytes 524320 | tf_op jit(solution)/shard_map/ppermute | solution.py:197
  342.1 9.4 %collective-permute-done.54 = bf16[128,2048]{1,0:T(8,128)(2,1)S(1)} collective-permute-done((bf16[128,2048]{1,0:T(8,128)(2,1)S(1)}, bf16[128,2048]{1,0:T(8,128)(2,1)S(1)}, u32[]{:S(2)}, u32[]{:S(2)}) %collective-permute-start.54) | collective-permute-done | bytes 524320 | tf_op jit(solution)/shard_map/ppermute | solution.py:197
  356.3 10.3 %collective-permute-done.55 = bf16[128,2048]{1,0:T(8,128)(2,1)S(1)} collective-permute-done((bf16[128,2048]{1,0:T(8,128)(2,1)S(1)}, bf16[128,2048]{1,0:T(8,128)(2,1)S(1)}, u32[]{:S(2)}, u32[]{:S(2)}) %collective-permute-start.55) | collective-permute-done | bytes 524320 | tf_op jit(solution)/shard_map/ppermute | solution.py:197
  372.1 12.3 %collective-permute-done.59 = bf16[128,2048]{1,0:T(8,128)(2,1)S(1)} collective-permute-done((bf16[128,2048]{1,0:T(8,128)(2,1)S(1)}, bf16[128,2048]{1,0:T(8,128)(2,1)S(1)}, u32[]{:S(2)}, u32[]{:S(2)}) %collective-permute-start.59) | collective-permute-done | bytes 524320 | tf_op jit(solution)/shard_map/ppermute | solution.py:197
  387.5 9.5 %collective-permute-done.61 = bf16[128,2048]{1,0:T(8,128)(2,1)} collective-permute-done((bf16[128,2048]{1,0:T(8,128)(2,1)}, bf16[128,2048]{1,0:T(8,128)(2,1)}, u32[]{:S(2)}, u32[]{:S(2)}) %collective-permute-start.61) | collective-permute-done | bytes 524320 | tf_op jit(solution)/shard_map/ppermute | solution.py:197
  399.0 7.7 fusion.145
  424.0 20.5 %collective-permute-done.65 = bf16[128,2048]{1,0:T(8,128)(2,1)S(1)} collective-permute-done((bf16[128,2048]{1,0:T(8,128)(2,1)S(1)}, bf16[128,2048]{1,0:T(8,128)(2,1)S(1)}, u32[]{:S(2)}, u32[]{:S(2)}) %collective-permute-start.65) | collective-permute-done | bytes 524320 | tf_op jit(solution)/shard_map/ppermute | solution.py:197
  450.1 7.1 collective-permute-done.66
  465.0 7.0 collective-permute-done.69
  473.0 5.3 add_convert_fusion.3
  487.7 8.7 %collective-permute-done.68 = bf16[128,2048]{1,0:T(8,128)(2,1)S(1)} collective-permute-done((bf16[128,2048]{1,0:T(8,128)(2,1)S(1)}, bf16[128,2048]{1,0:T(8,128)(2,1)S(1)}, u32[]{:S(2)}, u32[]{:S(2)}) %collective-permute-start.68) | collective-permute-done | bytes 524320 | tf_op jit(solution)/shard_map/ppermute | solution.py:197
  507.9 4.6 convert_add_fusion
  519.6 5.4 collective-permute-done.74
  539.7 5.6 collective-permute-done.78
  550.1 7.2 collective-permute-done.79
  563.1 15.7 %collective-permute-done.83 = bf16[2048,512]{1,0:T(8,128)(2,1)} collective-permute-done((bf16[2048,512]{1,0:T(8,128)(2,1)}, bf16[2048,512]{1,0:T(8,128)(2,1)}, u32[]{:S(2)}, u32[]{:S(2)}) %collective-permute-start.83) | collective-permute-done | bytes 2097184 | tf_op jit(solution)/shard_map/ppermute | solution.py:244
  578.7 5.0 add_convert_fusion.1
  588.2 10.0 %shard_map.189 = (f32[1024,512]{1,0:T(8,128)S(1)}, bf16[1024,256]{1,0:T(8,128)(2,1)S(1)}, f32[8,2,128]{2,1,0:T(2,128)S(1)}, f32[2,256]{1,0:T(2,128)S(1)}) custom-call(bf16[1024,768]{1,0:T(8,128)(2,1)S(1)} %get-tuple-element.95.rot_ref, bf16[1024,256]{1,0:T(8,128)(2,1)S(1)} %convolution_convert_fusion.4.up_ref, f32[1024,768]{1,0:T(8,128)S(1)} %copy-done.2, ...), custom_call_target="tpu_custom_call" | custom-call | flops 335544320 | bytes 7864320 | tf_op jit(solution)/shard_map/pallas_call | solution.py:645
  605.2 12.9 %collective-permute-done.110 = f32[4,2048]{1,0:T(4,128)S(1)} collective-permute-done((f32[4,2048]{1,0:T(4,128)S(1)}, f32[4,2048]{1,0:T(4,128)S(1)}, u32[]{:S(2)}, u32[]{:S(2)}) %collective-permute-start.110) | collective-permute-done | bytes 32800 | tf_op jit(solution)/shard_map/ppermute | solution.py:244
  634.1 5.2 all-to-all-start.1
  651.1 34.3 %collective-permute-done.114 = f32[4,2048]{1,0:T(4,128)S(1)} collective-permute-done((f32[4,2048]{1,0:T(4,128)S(1)}, f32[4,2048]{1,0:T(4,128)S(1)}, u32[]{:S(2)}, u32[]{:S(2)}) %collective-permute-start.114) | collective-permute-done | bytes 32800 | tf_op jit(solution)/shard_map/ppermute | solution.py:197
  699.1 5.8 collective-permute-done.92
  720.3 4.6 collective-permute-start.96
  755.6 31.6 %collective-permute-done.119.refs_2_ = bf16[8,256,512]{2,1,0:T(8,128)(2,1)S(1)} collective-permute-done((bf16[8,256,512]{2,1,0:T(8,128)(2,1)S(1)}, bf16[8,256,512]{2,1,0:T(8,128)(2,1)S(1)}, u32[]{:S(2)}, u32[]{:S(2)}) %collective-permute-start.119) | collective-permute-done | bytes 2097184 | tf_op jit(solution)/shard_map/ppermute | solution.py:244
  796.9 11.1 %collective-permute-done.116.refs_2_ = bf16[8,64,768]{2,1,0:T(8,128)(2,1)S(1)} collective-permute-done((bf16[8,64,768]{2,1,0:T(8,128)(2,1)S(1)}, bf16[8,64,768]{2,1,0:T(8,128)(2,1)S(1)}, u32[]{:S(2)}, u32[]{:S(2)}) %collective-permute-start.116) | collective-permute-done | bytes 786464 | tf_op jit(solution)/shard_map/ppermute | solution.py:244
  813.4 9.1 %shard_map.194 = f32[256,16384]{1,0:T(8,128)} custom-call(s32[1]{0:T(128)} %bitcast.56.copy_ref, bf16[8,256,512]{2,1,0:T(8,128)(2,1)S(1)} %all-to-all-done.1.refs_0_, bf16[8,256,512]{2,1,0:T(8,128)(2,1)S(1)} %collective-permute-done.118.refs_1_, bf16[8,256,512]{2,1,0:T(8,128)(2,1)S(1)} %collective-permute-done.119.refs_2_, ...), custom_call_target="tpu_custom_call" | custom-call | bytes 25165824 | tf_op jit(solution)/shard_map/pallas_call | solution.py:690
  (578 shorter events, 369.2 us)
Async XLA Ops:
  0.7 21.3 %collective-permute-start.1 = (bf16[128,2048]{1,0:T(8,128)(2,1)}, bf16[128,2048]{1,0:T(8,128)(2,1)S(1)}, u32[]{:S(2)}, u32[]{:S(2)}) collective-permute-start(bf16[128,2048]{1,0:T(8,128)(2,1)} %param.13), channel_id=1, source_target_pairs={{0,2},{1,3},{2,0},{3,1},{4,6},{5,7},{6,4},{7,5},{8,10},{9,11},{10,... | collective-permute-start | bytes 1572872 | tf_op jit(solution)/shard_map/ppermute | solution.py:197
  3.8 26.1 %collective-permute-start = (bf16[128,2048]{1,0:T(8,128)(2,1)}, bf16[128,2048]{1,0:T(8,128)(2,1)S(1)}, u32[]{:S(2)}, u32[]{:S(2)}) collective-permute-start(bf16[128,2048]{1,0:T(8,128)(2,1)} %param.13), channel_id=1, source_target_pairs={{0,1},{1,0},{2,3},{3,2},{4,5},{5,4},{6,7},{7,6},{8,9},{9,8},{10,11... | collective-permute-start | bytes 1572872 | tf_op jit(solution)/shard_map/ppermute | solution.py:197
  5.3 18.1 %collective-permute-start.2 = (bf16[128,2048]{1,0:T(8,128)(2,1)}, bf16[128,2048]{1,0:T(8,128)(2,1)S(1)}, u32[]{:S(2)}, u32[]{:S(2)}) collective-permute-start(bf16[128,2048]{1,0:T(8,128)(2,1)} %param.13), channel_id=1, source_target_pairs={{2,4},{3,5},{4,2},{5,3},{10,12},{11,13},{12,10},{13,11},{18,20},{1... | collective-permute-start | bytes 1572872 | tf_op jit(solution)/shard_map/ppermute | solution.py:201
  8.5 26.0 %collective-permute-start.6 = (bf16[64,768]{1,0:T(8,128)(2,1)}, bf16[64,768]{1,0:T(8,128)(2,1)}, u32[]{:S(2)}, u32[]{:S(2)}) collective-permute-start(bf16[64,768]{1,0:T(8,128)(2,1)} %pad_maximum_fusion.10), channel_id=1, source_target_pairs={{0,2},{1,3},{2,0},{3,1},{4,6},{5,7},{6,4},{7,5},{8,10},{9,11},{10,... | collective-permute-start | bytes 294920 | tf_op jit(solution)/shard_map/ppermute | solution.py:197
  13.5 22.4 %collective-permute-start.7 = (bf16[64,768]{1,0:T(8,128)(2,1)}, bf16[64,768]{1,0:T(8,128)(2,1)}, u32[]{:S(2)}, u32[]{:S(2)}) collective-permute-start(bf16[64,768]{1,0:T(8,128)(2,1)} %pad_maximum_fusion.11), channel_id=1, source_target_pairs={{0,3},{1,2},{2,1},{3,0},{4,7},{5,6},{6,5},{7,4},{8,11},{9,10},{10,... | collective-permute-start | bytes 294920 | tf_op jit(solution)/shard_map/ppermute | solution.py:197
  41.6 20.7 %collective-permute-start.12 = (bf16[128,2048]{1,0:T(8,128)(2,1)S(1)}, bf16[128,2048]{1,0:T(8,128)(2,1)S(1)}, u32[]{:S(2)}, u32[]{:S(2)}) collective-permute-start(bf16[128,2048]{1,0:T(8,128)(2,1)S(1)} %copy-done.53), channel_id=1, source_target_pairs={{4,6},{5,7},{2,0},{3,1},{12,14},{13,15},{10,8},{11,9},{20,22},{21,... | collective-permute-start | bytes 1572872 | tf_op jit(solution)/shard_map/ppermute | solution.py:201
  45.9 34.1 %collective-permute-start.17 = (bf16[8,64,768]{2,1,0:T(8,128)(2,1)S(1)}, bf16[8,64,768]{2,1,0:T(8,128)(2,1)S(1)}, u32[]{:S(2)}, u32[]{:S(2)}) collective-permute-start(bf16[8,64,768]{2,1,0:T(8,128)(2,1)S(1)} %bitcast_dynamic-update-slice_fusion.16), channel_id=1, source_target_pairs={{0,16},{8,24},{16,0},{24,8},{1,17},{9,25},{17,1},{25,9},{2,18},{10... | collective-permute-start | bytes 2359304 | tf_op jit(solution)/shard_map/ppermute | solution.py:244
  66.4 25.7 %collective-permute-start.14 = (bf16[128,2048]{1,0:T(8,128)(2,1)}, bf16[128,2048]{1,0:T(8,128)(2,1)}, u32[]{:S(2)}, u32[]{:S(2)}) collective-permute-start(bf16[128,2048]{1,0:T(8,128)(2,1)} %collective-permute-done.4), channel_id=1, source_target_pairs={{4,6},{5,7},{2,0},{3,1},{12,14},{13,15},{10,8},{11,9},{20,22},{21,... | collective-permute-start | bytes 1572872 | tf_op jit(solution)/shard_map/ppermute | solution.py:201
  68.5 97.9 %all-to-all-start = ((bf16[8,256,512]{2,1,0:T(8,128)(2,1)}), bf16[8,256,512]{2,1,0:T(8,128)(2,1)}, u32[]{:S(2)}, u32[]{:S(2)}) async-start(bf16[8,256,512]{2,1,0:T(8,128)(2,1)} %fusion.101), calls=%async_computation | async-start | bytes 4194304 | tf_op jit(solution)/shard_map/all_to_all | solution.py:539
  74.2 26.1 %collective-permute-start.16 = (bf16[8,64,768]{2,1,0:T(8,128)(2,1)S(1)}, bf16[8,64,768]{2,1,0:T(8,128)(2,1)S(1)}, u32[]{:S(2)}, u32[]{:S(2)}) collective-permute-start(bf16[8,64,768]{2,1,0:T(8,128)(2,1)S(1)} %bitcast_dynamic-update-slice_fusion.16), channel_id=1, source_target_pairs={{0,8},{8,0},{16,24},{24,16},{1,9},{9,1},{17,25},{25,17},{2,10},{10... | collective-permute-start | bytes 2359304 | tf_op jit(solution)/shard_map/ppermute | solution.py:240
  80.1 32.5 %collective-permute-start.18 = (bf16[8,64,768]{2,1,0:T(8,128)(2,1)S(1)}, bf16[8,64,768]{2,1,0:T(8,128)(2,1)S(1)}, u32[]{:S(2)}, u32[]{:S(2)}) collective-permute-start(bf16[8,64,768]{2,1,0:T(8,128)(2,1)S(1)} %collective-permute-done.17), channel_id=1, source_target_pairs={{0,8},{8,0},{16,24},{24,16},{1,9},{9,1},{17,25},{25,17},{2,10},{10... | collective-permute-start | bytes 2359304 | tf_op jit(solution)/shard_map/ppermute | solution.py:240
  93.3 19.2 %collective-permute-start.15 = (bf16[128,2048]{1,0:T(8,128)(2,1)S(1)}, bf16[128,2048]{1,0:T(8,128)(2,1)S(1)}, u32[]{:S(2)}, u32[]{:S(2)}) collective-permute-start(bf16[128,2048]{1,0:T(8,128)(2,1)S(1)} %get-tuple-element.153), channel_id=1, source_target_pairs={{0,1},{1,0},{2,3},{3,2},{4,5},{5,4},{6,7},{7,6},{8,9},{9,8},{10,11... | collective-permute-start | bytes 1572872 | tf_op jit(solution)/shard_map/ppermute | solution.py:197
  166.4 30.4 %collective-permute-start.37 = (bf16[2048,512]{1,0:T(8,128)(2,1)}, bf16[2048,512]{1,0:T(8,128)(2,1)S(1)}, u32[]{:S(2)}, u32[]{:S(2)}) collective-permute-start(bf16[2048,512]{1,0:T(8,128)(2,1)} %bitcast.31), channel_id=1, source_target_pairs={{0,16},{8,24},{16,0},{24,8},{1,17},{9,25},{17,1},{25,9},{2,18},{10... | collective-permute-start | bytes 6291464 | tf_op jit(solution)/shard_map/ppermute | solution.py:244
  174.9 21.9 %collective-permute-start.23 = (bf16[128,2048]{1,0:T(8,128)(2,1)S(1)}, bf16[128,2048]{1,0:T(8,128)(2,1)S(1)}, u32[]{:S(2)}, u32[]{:S(2)}) collective-permute-start(bf16[128,2048]{1,0:T(8,128)(2,1)S(1)} %slice.771), channel_id=1, source_target_pairs={{0,1},{1,0},{2,3},{3,2},{4,5},{5,4},{6,7},{7,6},{8,9},{9,8},{10,11... | collective-permute-start | bytes 1572872 | tf_op jit(solution)/shard_map/ppermute | solution.py:197
  176.3 20.5 %collective-permute-start.27 = (bf16[128,2048]{1,0:T(8,128)(2,1)S(1)}, bf16[128,2048]{1,0:T(8,128)(2,1)S(1)}, u32[]{:S(2)}, u32[]{:S(2)}) collective-permute-start(bf16[128,2048]{1,0:T(8,128)(2,1)S(1)} %copy-done.57), channel_id=1, source_target_pairs={{2,4},{3,5},{4,2},{5,3},{10,12},{11,13},{12,10},{13,11},{18,20},{1... | collective-permute-start | bytes 1572872 | tf_op jit(solution)/shard_map/ppermute | solution.py:201
  177.9 18.9 %collective-permute-start.31 = (bf16[128,2048]{1,0:T(8,128)(2,1)S(1)}, bf16[128,2048]{1,0:T(8,128)(2,1)S(1)}, u32[]{:S(2)}, u32[]{:S(2)}) collective-permute-start(bf16[128,2048]{1,0:T(8,128)(2,1)S(1)} %fusion.27), channel_id=1, source_target_pairs={{0,2},{1,3},{2,0},{3,1},{4,6},{5,7},{6,4},{7,5},{8,10},{9,11},{10,... | collective-permute-start | bytes 1572872 | tf_op jit(solution)/shard_map/ppermute | solution.py:197
  187.5 37.9 %collective-permute-start.36 = (bf16[2048,512]{1,0:T(8,128)(2,1)}, bf16[2048,512]{1,0:T(8,128)(2,1)S(1)}, u32[]{:S(2)}, u32[]{:S(2)}) collective-permute-start(bf16[2048,512]{1,0:T(8,128)(2,1)} %bitcast.31), channel_id=1, source_target_pairs={{0,8},{8,0},{16,24},{24,16},{1,9},{9,1},{17,25},{25,17},{2,10},{10... | collective-permute-start | bytes 6291464 | tf_op jit(solution)/shard_map/ppermute | solution.py:240
  196.8 28.6 %collective-permute-start.38 = (bf16[2048,512]{1,0:T(8,128)(2,1)S(1)}, bf16[2048,512]{1,0:T(8,128)(2,1)S(1)}, u32[]{:S(2)}, u32[]{:S(2)}) collective-permute-start(bf16[2048,512]{1,0:T(8,128)(2,1)S(1)} %collective-permute-done.37), channel_id=1, source_target_pairs={{0,8},{8,0},{16,24},{24,16},{1,9},{9,1},{17,25},{25,17},{2,10},{10... | collective-permute-start | bytes 6291464 | tf_op jit(solution)/shard_map/ppermute | solution.py:240
  225.4 20.5 %collective-permute-start.42 = (bf16[128,2048]{1,0:T(8,128)(2,1)S(1)}, bf16[128,2048]{1,0:T(8,128)(2,1)S(1)}, u32[]{:S(2)}, u32[]{:S(2)}) collective-permute-start(bf16[128,2048]{1,0:T(8,128)(2,1)S(1)} %collective-permute-done.35), channel_id=1, source_target_pairs={{4,6},{5,7},{2,0},{3,1},{12,14},{13,15},{10,8},{11,9},{20,22},{21,... | collective-permute-start | bytes 1572872 | tf_op jit(solution)/shard_map/ppermute | solution.py:201
  275.3 18.7 %collective-permute-start.45 = (bf16[128,2048]{1,0:T(8,128)(2,1)S(1)}, bf16[128,2048]{1,0:T(8,128)(2,1)S(1)}, u32[]{:S(2)}, u32[]{:S(2)}) collective-permute-start(bf16[128,2048]{1,0:T(8,128)(2,1)S(1)} %slice.766), channel_id=1, source_target_pairs={{0,1},{1,0},{2,3},{3,2},{4,5},{5,4},{6,7},{7,6},{8,9},{9,8},{10,11... | collective-permute-start | bytes 1572872 | tf_op jit(solution)/shard_map/ppermute | solution.py:197
  318.7 18.1 %collective-permute-start.52 = (bf16[128,2048]{1,0:T(8,128)(2,1)S(1)}, bf16[128,2048]{1,0:T(8,128)(2,1)S(1)}, u32[]{:S(2)}, u32[]{:S(2)}) collective-permute-start(bf16[128,2048]{1,0:T(8,128)(2,1)S(1)} %fusion.23), channel_id=1, source_target_pairs={{0,2},{1,3},{2,0},{3,1},{4,6},{5,7},{6,4},{7,5},{8,10},{9,11},{10,... | collective-permute-start | bytes 1572872 | tf_op jit(solution)/shard_map/ppermute | solution.py:197
  416.4 56.6 %collective-permute-start.62 = (bf16[512,2048]{1,0:T(8,128)(2,1)}, bf16[512,2048]{1,0:T(8,128)(2,1)}, u32[]{:S(2)}, u32[]{:S(2)}) collective-permute-start(bf16[512,2048]{1,0:T(8,128)(2,1)} %convolution_convert_fusion.2), channel_id=1, source_target_pairs={{0,8},{8,0},{16,24},{24,16},{1,9},{9,1},{17,25},{25,17},{2,10},{10... | collective-permute-start | bytes 6291464 | tf_op jit(solution)/shard_map/ppermute | solution.py:240
  418.8 31.2 %collective-permute-start.64 = (bf16[128,2048]{1,0:T(8,128)(2,1)S(1)}, bf16[128,2048]{1,0:T(8,128)(2,1)S(1)}, u32[]{:S(2)}, u32[]{:S(2)}) collective-permute-start(bf16[128,2048]{1,0:T(8,128)(2,1)S(1)} %slice.762), channel_id=1, source_target_pairs={{0,1},{1,0},{2,3},{3,2},{4,5},{5,4},{6,7},{7,6},{8,9},{9,8},{10,11... | collective-permute-start | bytes 1572872 | tf_op jit(solution)/shard_map/ppermute | solution.py:197
  421.3 23.1 %collective-permute-start.65 = (bf16[128,2048]{1,0:T(8,128)(2,1)S(1)}, bf16[128,2048]{1,0:T(8,128)(2,1)S(1)}, u32[]{:S(2)}, u32[]{:S(2)}) collective-permute-start(bf16[128,2048]{1,0:T(8,128)(2,1)S(1)} %slice.761), channel_id=1, source_target_pairs={{0,1},{1,0},{2,3},{3,2},{4,5},{5,4},{6,7},{7,6},{8,9},{9,8},{10,11... | collective-permute-start | bytes 1572872 | tf_op jit(solution)/shard_map/ppermute | solution.py:197
  464.3 36.0 %collective-permute-start.67 = (bf16[128,2048]{1,0:T(8,128)(2,1)S(1)}, bf16[128,2048]{1,0:T(8,128)(2,1)S(1)}, u32[]{:S(2)}, u32[]{:S(2)}) collective-permute-start(bf16[128,2048]{1,0:T(8,128)(2,1)S(1)} %get-tuple-element.214), channel_id=1, source_target_pairs={{2,4},{3,5},{4,2},{5,3},{10,12},{11,13},{12,10},{13,11},{18,20},{1... | collective-permute-start | bytes 1572872 | tf_op jit(solution)/shard_map/ppermute | solution.py:201
  484.7 23.2 %collective-permute-start.72 = (bf16[2048,512]{1,0:T(8,128)(2,1)S(1)}, bf16[2048,512]{1,0:T(8,128)(2,1)S(1)}, u32[]{:S(2)}, u32[]{:S(2)}) collective-permute-start(bf16[2048,512]{1,0:T(8,128)(2,1)S(1)} %copy-done.77), channel_id=1, source_target_pairs={{0,8},{8,0},{16,24},{24,16},{1,9},{9,1},{17,25},{25,17},{2,10},{10... | collective-permute-start | bytes 6291464 | tf_op jit(solution)/shard_map/ppermute | solution.py:240
  486.5 18.2 %collective-permute-start.63 = (bf16[128,2048]{1,0:T(8,128)(2,1)S(1)}, bf16[128,2048]{1,0:T(8,128)(2,1)S(1)}, u32[]{:S(2)}, u32[]{:S(2)}) collective-permute-start(bf16[128,2048]{1,0:T(8,128)(2,1)S(1)} %slice.763), channel_id=1, source_target_pairs={{0,1},{1,0},{2,3},{3,2},{4,5},{5,4},{6,7},{7,6},{8,9},{9,8},{10,11... | collective-permute-start | bytes 1572872 | tf_op jit(solution)/shard_map/ppermute | solution.py:197
  500.3 25.7 %collective-permute-start.82 = (bf16[2048,512]{1,0:T(8,128)(2,1)S(1)}, bf16[2048,512]{1,0:T(8,128)(2,1)S(1)}, u32[]{:S(2)}, u32[]{:S(2)}) collective-permute-start(bf16[2048,512]{1,0:T(8,128)(2,1)S(1)} %convolution_convert_fusion.1), channel_id=1, source_target_pairs={{0,8},{8,0},{16,24},{24,16},{1,9},{9,1},{17,25},{25,17},{2,10},{10... | collective-permute-start | bytes 6291464 | tf_op jit(solution)/shard_map/ppermute | solution.py:240
  529.9 48.8 %collective-permute-start.83 = (bf16[2048,512]{1,0:T(8,128)(2,1)}, bf16[2048,512]{1,0:T(8,128)(2,1)}, u32[]{:S(2)}, u32[]{:S(2)}) collective-permute-start(bf16[2048,512]{1,0:T(8,128)(2,1)} %add_convert_fusion.2), channel_id=1, source_target_pairs={{0,16},{8,24},{16,0},{24,8},{1,17},{9,25},{17,1},{25,9},{2,18},{10... | collective-permute-start | bytes 6291464 | tf_op jit(solution)/shard_map/ppermute | solution.py:244
  549.5 97.6 %collective-permute-start.121 = (bf16[512,2048]{1,0:T(8,128)(2,1)}, bf16[512,2048]{1,0:T(8,128)(2,1)}, u32[]{:S(2)}, u32[]{:S(2)}) collective-permute-start(bf16[512,2048]{1,0:T(8,128)(2,1)} %add_convert_fusion.3), channel_id=1, source_target_pairs={{0,16},{8,24},{16,0},{24,8},{1,17},{9,25},{17,1},{25,9},{2,18},{10... | collective-permute-start | bytes 6291464 | tf_op jit(solution)/shard_map/ppermute | solution.py:244
  561.7 22.0 %collective-permute-start.81 = (bf16[128,2048]{1,0:T(8,128)(2,1)S(1)}, bf16[128,2048]{1,0:T(8,128)(2,1)S(1)}, u32[]{:S(2)}, u32[]{:S(2)}) collective-permute-start(bf16[128,2048]{1,0:T(8,128)(2,1)S(1)} %get-tuple-element.131), channel_id=1, source_target_pairs={{0,1},{1,0},{2,3},{3,2},{4,5},{5,4},{6,7},{7,6},{8,9},{9,8},{10,11... | collective-permute-start | bytes 1572872 | tf_op jit(solution)/shard_map/ppermute | solution.py:197
  599.6 18.5 %collective-permute-start.110 = (f32[4,2048]{1,0:T(4,128)S(1)}, f32[4,2048]{1,0:T(4,128)S(1)}, u32[]{:S(2)}, u32[]{:S(2)}) collective-permute-start(f32[4,2048]{1,0:T(4,128)S(1)} %pad_maximum_fusion.17), channel_id=1, source_target_pairs={{0,16},{8,24},{16,0},{24,8},{1,17},{9,25},{17,1},{25,9},{2,18},{10... | collective-permute-start | bytes 98312 | tf_op jit(solution)/shard_map/ppermute | solution.py:244
  605.2 37.2 %collective-permute-start.88 = (bf16[128,2048]{1,0:T(8,128)(2,1)}, bf16[128,2048]{1,0:T(8,128)(2,1)}, u32[]{:S(2)}, u32[]{:S(2)}) collective-permute-start(bf16[128,2048]{1,0:T(8,128)(2,1)} %convolution_convert_fusion.3), channel_id=1, source_target_pairs={{0,8},{8,0},{16,24},{24,16},{1,9},{9,1},{17,25},{25,17},{2,10},{10... | collective-permute-start | bytes 1572872 | tf_op jit(solution)/shard_map/ppermute | solution.py:240
  634.1 110.7 %all-to-all-start.1 = ((bf16[8,256,512]{2,1,0:T(8,128)(2,1)}), bf16[8,256,512]{2,1,0:T(8,128)(2,1)S(1)}, u32[]{:S(2)}, u32[]{:S(2)}) async-start(bf16[8,256,512]{2,1,0:T(8,128)(2,1)} %bitcast.240), calls=%async_computation.1 | async-start | bytes 4194304 | tf_op jit(solution)/shard_map/all_to_all | solution.py:630
  639.4 46.1 %collective-permute-start.114 = (f32[4,2048]{1,0:T(4,128)S(1)}, f32[4,2048]{1,0:T(4,128)S(1)}, u32[]{:S(2)}, u32[]{:S(2)}) collective-permute-start(f32[4,2048]{1,0:T(4,128)S(1)} %add.802), channel_id=1, source_target_pairs={{0,4},{1,5},{2,6},{3,7},{4,0},{5,1},{6,2},{7,3},{8,12},{9,13},{10,... | collective-permute-start | bytes 98312 | tf_op jit(solution)/shard_map/ppermute | solution.py:197
  645.5 39.9 %collective-permute-start.89 = (bf16[128,2048]{1,0:T(8,128)(2,1)S(1)}, bf16[128,2048]{1,0:T(8,128)(2,1)S(1)}, u32[]{:S(2)}, u32[]{:S(2)}) collective-permute-start(bf16[128,2048]{1,0:T(8,128)(2,1)S(1)} %fusion), channel_id=1, source_target_pairs={{0,16},{8,24},{16,0},{24,8},{1,17},{9,25},{17,1},{25,9},{2,18},{10... | collective-permute-start | bytes 1572872 | tf_op jit(solution)/shard_map/ppermute | solution.py:244
  649.7 82.4 %collective-permute-start.122 = (bf16[512,2048]{1,0:T(8,128)(2,1)S(1)}, bf16[512,2048]{1,0:T(8,128)(2,1)S(1)}, u32[]{:S(2)}, u32[]{:S(2)}) collective-permute-start(bf16[512,2048]{1,0:T(8,128)(2,1)S(1)} %add_convert_fusion), channel_id=1, source_target_pairs={{0,8},{8,0},{16,24},{24,16},{1,9},{9,1},{17,25},{25,17},{2,10},{10... | collective-permute-start | bytes 6291464 | tf_op jit(solution)/shard_map/ppermute | solution.py:240
  696.6 28.3 %collective-permute-start.99 = (bf16[8,64,768]{2,1,0:T(8,128)(2,1)S(1)}, bf16[8,64,768]{2,1,0:T(8,128)(2,1)S(1)}, u32[]{:S(2)}, u32[]{:S(2)}) collective-permute-start(bf16[8,64,768]{2,1,0:T(8,128)(2,1)S(1)} %get-tuple-element.108), channel_id=1, source_target_pairs={{0,8},{8,0},{16,24},{24,16},{1,9},{9,1},{17,25},{25,17},{2,10},{10... | collective-permute-start | bytes 2359304 | tf_op jit(solution)/shard_map/ppermute | solution.py:240
  709.4 18.1 %collective-permute-start.101 = (bf16[8,64,768]{2,1,0:T(8,128)(2,1)S(1)}, bf16[8,64,768]{2,1,0:T(8,128)(2,1)S(1)}, u32[]{:S(2)}, u32[]{:S(2)}) collective-permute-start(bf16[8,64,768]{2,1,0:T(8,128)(2,1)S(1)} %fusion.1), channel_id=1, source_target_pairs={{0,16},{8,24},{16,0},{24,8},{1,17},{9,25},{17,1},{25,9},{2,18},{10... | collective-permute-start | bytes 2359304 | tf_op jit(solution)/shard_map/ppermute | solution.py:244
  720.3 18.2 %collective-permute-start.96 = (bf16[128,2048]{1,0:T(8,128)(2,1)S(1)}, bf16[128,2048]{1,0:T(8,128)(2,1)S(1)}, u32[]{:S(2)}, u32[]{:S(2)}) collective-permute-start(bf16[128,2048]{1,0:T(8,128)(2,1)S(1)} %get-tuple-element.213), channel_id=1, source_target_pairs={{6,4},{7,5},{0,2},{1,3},{14,12},{15,13},{8,10},{9,11},{22,20},{23,... | collective-permute-start | bytes 1572872 | tf_op jit(solution)/shard_map/ppermute | solution.py:201
  744.8 42.4 %collective-permute-start.119 = (bf16[8,256,512]{2,1,0:T(8,128)(2,1)S(1)}, bf16[8,256,512]{2,1,0:T(8,128)(2,1)S(1)}, u32[]{:S(2)}, u32[]{:S(2)}) collective-permute-start(bf16[8,256,512]{2,1,0:T(8,128)(2,1)S(1)} %all-to-all-done.1.refs_0_), channel_id=1, source_target_pairs={{0,16},{8,24},{16,0},{24,8},{1,17},{9,25},{17,1},{25,9},{2,18},{10... | collective-permute-start | bytes 6291464 | tf_op jit(solution)/shard_map/ppermute | solution.py:244
  748.1 39.2 %collective-permute-start.95 = (bf16[128,2048]{1,0:T(8,128)(2,1)}, bf16[128,2048]{1,0:T(8,128)(2,1)S(1)}, u32[]{:S(2)}, u32[]{:S(2)}) collective-permute-start(bf16[128,2048]{1,0:T(8,128)(2,1)} %slice.756), channel_id=1, source_target_pairs={{0,1},{1,0},{2,3},{3,2},{4,5},{5,4},{6,7},{7,6},{8,9},{9,8},{10,11... | collective-permute-start | bytes 1572872 | tf_op jit(solution)/shard_map/ppermute | solution.py:197
  749.6 40.1 %collective-permute-start.90 = (bf16[128,2048]{1,0:T(8,128)(2,1)}, bf16[128,2048]{1,0:T(8,128)(2,1)S(1)}, u32[]{:S(2)}, u32[]{:S(2)}) collective-permute-start(bf16[128,2048]{1,0:T(8,128)(2,1)} %slice.759), channel_id=1, source_target_pairs={{0,1},{1,0},{2,3},{3,2},{4,5},{5,4},{6,7},{7,6},{8,9},{9,8},{10,11... | collective-permute-start | bytes 1572872 | tf_op jit(solution)/shard_map/ppermute | solution.py:197
  750.2 37.8 %collective-permute-start.97 = (bf16[128,2048]{1,0:T(8,128)(2,1)S(1)}, bf16[128,2048]{1,0:T(8,128)(2,1)S(1)}, u32[]{:S(2)}, u32[]{:S(2)}) collective-permute-start(bf16[128,2048]{1,0:T(8,128)(2,1)S(1)} %add_convert_fusion.5), channel_id=1, source_target_pairs={{2,4},{3,5},{4,2},{5,3},{10,12},{11,13},{12,10},{13,11},{18,20},{1... | collective-permute-start | bytes 1572872 | tf_op jit(solution)/shard_map/ppermute | solution.py:201
  755.5 57.9 %collective-permute-start.118 = (bf16[8,256,512]{2,1,0:T(8,128)(2,1)S(1)}, bf16[8,256,512]{2,1,0:T(8,128)(2,1)S(1)}, u32[]{:S(2)}, u32[]{:S(2)}) collective-permute-start(bf16[8,256,512]{2,1,0:T(8,128)(2,1)S(1)} %all-to-all-done.1.refs_0_), channel_id=1, source_target_pairs={{0,8},{8,0},{16,24},{24,16},{1,9},{9,1},{17,25},{25,17},{2,10},{10... | collective-permute-start | bytes 6291464 | tf_op jit(solution)/shard_map/ppermute | solution.py:240
  787.3 26.1 %collective-permute-start.120 = (bf16[8,256,512]{2,1,0:T(8,128)(2,1)S(1)}, bf16[8,256,512]{2,1,0:T(8,128)(2,1)S(1)}, u32[]{:S(2)}, u32[]{:S(2)}) collective-permute-start(bf16[8,256,512]{2,1,0:T(8,128)(2,1)S(1)} %collective-permute-done.119.refs_2_), channel_id=1, source_target_pairs={{0,8},{8,0},{16,24},{24,16},{1,9},{9,1},{17,25},{25,17},{2,10},{10... | collective-permute-start | bytes 6291464 | tf_op jit(solution)/shard_map/ppermute | solution.py:240
  788.0 20.0 %collective-permute-start.116 = (bf16[8,64,768]{2,1,0:T(8,128)(2,1)S(1)}, bf16[8,64,768]{2,1,0:T(8,128)(2,1)S(1)}, u32[]{:S(2)}, u32[]{:S(2)}) collective-permute-start(bf16[8,64,768]{2,1,0:T(8,128)(2,1)S(1)} %bitcast_dynamic-update-slice_fusion.8.refs_0_), channel_id=1, source_target_pairs={{0,16},{8,24},{16,0},{24,8},{1,17},{9,25},{17,1},{25,9},{2,18},{10... | collective-permute-start | bytes 2359304 | tf_op jit(solution)/shard_map/ppermute | solution.py:244
  789.8 18.9 %collective-permute-start.98 = (bf16[128,2048]{1,0:T(8,128)(2,1)S(1)}, bf16[128,2048]{1,0:T(8,128)(2,1)S(1)}, u32[]{:S(2)}, u32[]{:S(2)}) collective-permute-start(bf16[128,2048]{1,0:T(8,128)(2,1)S(1)} %fusion.13), channel_id=1, source_target_pairs={{0,2},{1,3},{2,0},{3,1},{4,6},{5,7},{6,4},{7,5},{8,10},{9,11},{10,... | collective-permute-start | bytes 1572872 | tf_op jit(solution)/shard_map/ppermute | solution.py:197
  (157 other events, 2380.6 us)
where the time goes:
time: 834 us; the launch traced here: 823 us
  waiting for transfers between devices  407 us (49%)
  starting transfers between devices  191 us (23%)
  matrix products  82.2 us (10%)
  other arithmetic  57.7 us (7%)
  local copies, waits for them, and re-layouts  50.8 us (6%)
  Pallas kernels  30.3 us (4%)
    ppermute x65, waiting for transfers between devices, hop(): return lax.ppermute(value, 'fsdp', swap_pairs(8, bits))  252 us
    ppermute x65, starting transfers between devices, hop(): return lax.ppermute(value, 'fsdp', swap_pairs(8, bits))  114 us
    ppermute x9, waiting for transfers between devices, chip_hop(): return lax.ppermute(value, 'replica', swap_pairs(4, 2))  83.2 us
    ppermute x32, waiting for transfers between devices, lane(): return lax.ppermute(value, 'fsdp', lane_pairs(hops))  69.9 us
    ppermute x32, starting transfers between devices, lane(): return lax.ppermute(value, 'fsdp', lane_pairs(hops))  51.4 us
    dot_general x9, matrix products, tn(): return lax.dot_general(a, b, ROWS_DIMS, preferred_element_type=F32)  34.1 us
    dot_general x22, matrix products, back_with(): lax.dot_general(upstream, incoming, COLS_DIMS, preferred_element_type=jnp...  27.9 us
    unnamed x177, local copies, waits for them, and re-layouts  23.8 us
  transfers between devices with their start and end apart: 125, of which 57 were waited for; matrix products, arithmetic and copies ran while one was open for 17% of the time, Pallas kernels for 3%

commit v1 on v0

--- a/solution.py
+++ b/solution.py
@@ -569,10 +569,15 @@
         return far
 
     mid_all = jnp.concatenate(spread(mid_b, None, late_mid))
-    gate_up_cols = absolute(gate_up_all, copy)
-    gate_up = [fold_with(mid_all, gate_up_cols[c]) for c in range(copies)]
-    gate = [value[:, :quarter] for value in gate_up]
-    upper = [value[:, quarter:] for value in gate_up]
+    gate_up_cols = jnp.zeros((D, 2 * units), BF16)
+    for k, block in enumerate(gate_up_all):
+        gate_up_cols = lax.dynamic_update_slice_in_dim(
+            gate_up_cols, block, (copy ^ k) * 2 * quarter, axis=1
+        )
+    gate_up = fold_with(mid_all, gate_up_cols)
+    strip = lambda i: gate_up[:, i * quarter : (i + 1) * quarter]
+    gate = [strip(2 * c) for c in range(copies)]
+    upper = [strip(2 * c + 1) for c in range(copies)]
     sigma = [jax.nn.sigmoid(value) for value in gate]
     hidden_b = jnp.concatenate(
         [(g * s * u).astype(BF16) for g, s, u in zip(gate, sigma, upper)], axis=1
@@ -589,33 +594,28 @@
         d_h = d_hidden[:, c * quarter : (c + 1) * quarter]
         d_gate = d_h * upper[c] * sigma[c] * (1.0 + gate[c] * (1.0 - sigma[c]))
         d_upper = d_h * gate[c] * sigma[c]
-        dgu.append(jnp.concatenate([d_gate, d_upper], axis=1).astype(BF16))
-
-    def d_mid_part(j):
-        total = back_with(rows_of(dgu[0], j), gate_up_cols[0])
-        for c in range(1, copies):
-            total = total + back_with(rows_of(dgu[c], j), gate_up_cols[c])
-        return total.reshape(2, rows, D)
-
-    dgu_all = jnp.stack(dgu)
+        dgu += [d_gate.astype(BF16), d_upper.astype(BF16)]
+    dgu = jnp.concatenate(dgu, axis=1)
     quarter_grad = lambda m: tn(
-        mid_all, lax.dynamic_index_in_dim(dgu_all, copy ^ m, axis=0, keepdims=False)
-    )
+        mid_all, lax.dynamic_slice_in_dim(dgu_all, (copy ^ m) * 2 * quarter, 2 * quarter, axis=1)
+    )
+    dgu_all = dgu
     kept = {}
 
     def d_mid_step(j):
+        nonlocal dgu
         if j == 1:
             pair = halves(hidden_b, dmlp_all, core, units // 2)
-            dgu[0], kept["pair"] = tie((dgu[0], pair))
+            dgu, kept["pair"] = tie((dgu, pair))
             kept["down"] = chip_hop(kept["pair"])
         if j == 0:
             sends = [quarter_grad(m).astype(BF16) for m in (3, 1)]
-            dgu[0], *sends = tie((dgu[0], *sends))
+            dgu, *sends = tie((dgu, *sends))
             kept[3], kept[1] = (core_hop(value) for value in sends)
             sent = (quarter_grad(2) + kept[3].astype(F32)).astype(BF16)
             kept[2] = chip_hop(sent)
             kept[0] = quarter_grad(0) + kept[1].astype(F32)
-        return d_mid_part(j)
+        return back_with(rows_of(dgu, j), gate_up_cols).reshape(2, rows, D)
 
     d_mid = cotangent + collect(d_mid_step)
     d_mid, gate_up_own = tie((d_mid, kept[0]))

time: 834 us -> 846 us (1.014)
  waiting for transfers between devices: 407 us -> 381 us
  local copies, waits for them, and re-layouts: 50.8 us -> 64.8 us
  starting transfers between devices: 191 us -> 201 us
  matrix products: 82.2 us -> 91.2 us
    ppermute x32, waiting for transfers between devices: 69.9 us -> 54.2 us  [lane(): return lax.ppermute(value, 'fsdp', lane_pairs(hops))]
    ppermute x65, waiting for transfers between devices: 252 us -> 237 us  [hop(): return lax.ppermute(value, 'fsdp', swap_pairs(8, bits))]
    unnamed x19 -> x27, other arithmetic: 15.6 us -> 27.4 us
    ppermute x32, starting transfers between devices: 51.4 us -> 62.1 us  [lane(): return lax.ppermute(value, 'fsdp', lane_pairs(hops))]
    dot_general x9, matrix products: 34.1 us -> 43.8 us  [tn(): return lax.dot_general(a, b, ROWS_DIMS, preferred_element_type=F32)]
    unnamed x177 -> x151, local copies, waits for them, and re-layouts: 23.8 us -> 31.9 us
    dot_general x13 -> x10, matrix products: 20.2 us -> 19.3 us  [fold_with(): return jnp.dot(activations, incoming, preferred_element_type=jnp.float32)]
    dot_general x22 -> x10, matrix products: 27.9 us -> 28 us  [back_with(): lax.dot_general(upstream, incoming, COLS_DIMS, preferred_element_type=jnp...]
  transfers between devices with their start and end apart: 125 -> 125, of which waited for: 57 -> 56; matrix products, arithmetic and copies ran while one was open for 17% -> 21% of each run, Pallas kernels for 3% -> 3%
where the time goes in v1:
time: 846 us; the launch traced here: 835 us
  waiting for transfers between devices  381 us (45%)
  starting transfers between devices  201 us (24%)
  matrix products  91.2 us (11%)
  local copies, waits for them, and re-layouts  64.8 us (8%)
  other arithmetic  64.4 us (8%)
  Pallas kernels  30.4 us (4%)
    ppermute x65, waiting for transfers between devices, hop(): return lax.ppermute(value, 'fsdp', swap_pairs(8, bits))  237 us
    ppermute x65, starting transfers between devices, hop(): return lax.ppermute(value, 'fsdp', swap_pairs(8, bits))  113 us
    ppermute x9, waiting for transfers between devices, chip_hop(): return lax.ppermute(value, 'replica', swap_pairs(4, 2))  88.3 us
    ppermute x32, starting transfers between devices, lane(): return lax.ppermute(value, 'fsdp', lane_pairs(hops))  62.1 us
    ppermute x32, waiting for transfers between devices, lane(): return lax.ppermute(value, 'fsdp', lane_pairs(hops))  54.2 us
    dot_general x9, matrix products, tn(): return lax.dot_general(a, b, ROWS_DIMS, preferred_element_type=F32)  43.8 us
    unnamed x151, local copies, waits for them, and re-layouts  31.9 us
    dot_general x10, matrix products, back_with(): lax.dot_general(upstream, incoming, COLS_DIMS, preferred_element_type=jnp...  28 us
  transfers between devices with their start and end apart: 125, of which 56 were waited for; matrix products, arithmetic and copies ran while one was open for 21% of the time, Pallas kernels for 3%

profile of v1, /device:TPU:0, one launch (start us, length us, event | category | flops | bytes accessed | tf_op | source)
XLA Modules:
  0.0 835.4 jit_solution(15530709831122799798)
XLA Ops:
  45.9 5.8 collective-permute-done.3
  52.5 7.1 collective-permute-done.12
  65.9 6.7 all-to-all-start
  75.0 6.9 collective-permute-done.14
  83.0 5.8 collective-permute-start.15
  89.0 17.5 %collective-permute-done.15 = bf16[128,2048]{1,0:T(8,128)(2,1)S(1)} collective-permute-done((bf16[128,2048]{1,0:T(8,128)(2,1)S(1)}, bf16[128,2048]{1,0:T(8,128)(2,1)S(1)}, u32[]{:S(2)}, u32[]{:S(2)}) %collective-permute-start.15) | collective-permute-done | bytes 524320 | tf_op jit(solution)/shard_map/ppermute | solution.py:197
  114.3 5.9 collective-permute-start.22
  126.7 6.8 shard_map.188
  136.8 9.2 %collective-permute-done.25 = bf16[128,2048]{1,0:T(8,128)(2,1)S(1)} collective-permute-done((bf16[128,2048]{1,0:T(8,128)(2,1)S(1)}, bf16[128,2048]{1,0:T(8,128)(2,1)S(1)}, u32[]{:S(2)}, u32[]{:S(2)}) %collective-permute-start.25) | collective-permute-done | bytes 524320 | tf_op jit(solution)/shard_map/ppermute | solution.py:197
  151.6 7.8 collective-permute-done.26
  160.6 15.9 %collective-permute-start.29 = (bf16[128,2048]{1,0:T(8,128)(2,1)}, bf16[128,2048]{1,0:T(8,128)(2,1)}, u32[]{:S(2)}, u32[]{:S(2)}) collective-permute-start(bf16[128,2048]{1,0:T(8,128)(2,1)} %get-tuple-element.211), channel_id=1, source_target_pairs={{6,4},{7,5},{0,2},{1,3},{14,12},{15,13},{8,10},{9,11},{22,20},{23,... | collective-permute-start | bytes 1572872 | tf_op jit(solution)/shard_map/ppermute | solution.py:201
  191.8 15.2 %collective-permute-done.37 = bf16[2048,512]{1,0:T(8,128)(2,1)} collective-permute-done((bf16[2048,512]{1,0:T(8,128)(2,1)}, bf16[2048,512]{1,0:T(8,128)(2,1)}, u32[]{:S(2)}, u32[]{:S(2)}) %collective-permute-start.37) | collective-permute-done | bytes 2097184 | tf_op jit(solution)/shard_map/ppermute | solution.py:244
  212.7 11.6 %collective-permute-done.33 = bf16[128,2048]{1,0:T(8,128)(2,1)} collective-permute-done((bf16[128,2048]{1,0:T(8,128)(2,1)}, bf16[128,2048]{1,0:T(8,128)(2,1)}, u32[]{:S(2)}, u32[]{:S(2)}) %collective-permute-start.33) | collective-permute-done | bytes 524320 | tf_op jit(solution)/shard_map/ppermute | solution.py:197
  231.7 6.4 collective-permute-done.34
  252.1 5.2 collective-permute-done.41
  264.2 5.7 collective-permute-done.43
  270.0 8.8 %fusion.108 = f32[1024,2048]{1,0:T(8,128)S(1)} fusion(bf16[1024,2048]{1,0:T(8,128)(2,1)S(1)} %constant_dynamic-update-slice_fusion.8, bf16[2048,2048]{1,0:T(8,128)(2,1)S(1)} %constant_dynamic-update-slice_fusion.33), kind=kOutput, calls=%fused_computation.309 | convolution fusion | flops 8589934592 | bytes 20971520 | tf_op jit(solution)/shard_map/dot_general | solution.py:68
  289.3 11.4 %collective-permute-done.46 = bf16[128,2048]{1,0:T(8,128)(2,1)S(1)} collective-permute-done((bf16[128,2048]{1,0:T(8,128)(2,1)S(1)}, bf16[128,2048]{1,0:T(8,128)(2,1)S(1)}, u32[]{:S(2)}, u32[]{:S(2)}) %collective-permute-start.46) | collective-permute-done | bytes 524320 | tf_op jit(solution)/shard_map/ppermute | solution.py:197
  307.5 6.0 collective-permute-done.47
  313.7 4.6 collective-permute-start.50
  332.2 8.1 collective-permute-start.52
  340.3 10.7 %collective-permute-done.52 = bf16[128,2048]{1,0:T(8,128)(2,1)S(1)} collective-permute-done((bf16[128,2048]{1,0:T(8,128)(2,1)S(1)}, bf16[128,2048]{1,0:T(8,128)(2,1)S(1)}, u32[]{:S(2)}, u32[]{:S(2)}) %collective-permute-start.52) | collective-permute-done | bytes 524320 | tf_op jit(solution)/shard_map/ppermute | solution.py:197
  357.0 9.4 %collective-permute-done.54 = bf16[128,2048]{1,0:T(8,128)(2,1)S(1)} collective-permute-done((bf16[128,2048]{1,0:T(8,128)(2,1)S(1)}, bf16[128,2048]{1,0:T(8,128)(2,1)S(1)}, u32[]{:S(2)}, u32[]{:S(2)}) %collective-permute-start.54) | collective-permute-done | bytes 524320 | tf_op jit(solution)/shard_map/ppermute | solution.py:197
  372.9 8.7 %collective-permute-done.55 = bf16[128,2048]{1,0:T(8,128)(2,1)S(1)} collective-permute-done((bf16[128,2048]{1,0:T(8,128)(2,1)S(1)}, bf16[128,2048]{1,0:T(8,128)(2,1)S(1)}, u32[]{:S(2)}, u32[]{:S(2)}) %collective-permute-start.55) | collective-permute-done | bytes 524320 | tf_op jit(solution)/shard_map/ppermute | solution.py:197
  388.3 11.9 %collective-permute-done.59 = bf16[128,2048]{1,0:T(8,128)(2,1)S(1)} collective-permute-done((bf16[128,2048]{1,0:T(8,128)(2,1)S(1)}, bf16[128,2048]{1,0:T(8,128)(2,1)S(1)}, u32[]{:S(2)}, u32[]{:S(2)}) %collective-permute-start.59) | collective-permute-done | bytes 524320 | tf_op jit(solution)/shard_map/ppermute | solution.py:197
  402.6 9.0 %collective-permute-done.61 = bf16[128,2048]{1,0:T(8,128)(2,1)} collective-permute-done((bf16[128,2048]{1,0:T(8,128)(2,1)}, bf16[128,2048]{1,0:T(8,128)(2,1)}, u32[]{:S(2)}, u32[]{:S(2)}) %collective-permute-start.61) | collective-permute-done | bytes 524320 | tf_op jit(solution)/shard_map/ppermute | solution.py:197
  413.7 8.1 fusion.109
  421.8 5.9 convolution_convert_fusion.2
  444.1 10.3 %collective-permute-done.65 = bf16[128,2048]{1,0:T(8,128)(2,1)S(1)} collective-permute-done((bf16[128,2048]{1,0:T(8,128)(2,1)S(1)}, bf16[128,2048]{1,0:T(8,128)(2,1)S(1)}, u32[]{:S(2)}, u32[]{:S(2)}) %collective-permute-start.65) | collective-permute-done | bytes 524320 | tf_op jit(solution)/shard_map/ppermute | solution.py:197
  456.5 6.2 convolution_convert_fusion
  475.9 5.2 collective-permute-done.69
  482.0 6.0 add_convert_fusion.3
  497.8 8.9 %collective-permute-done.68 = bf16[128,2048]{1,0:T(8,128)(2,1)S(1)} collective-permute-done((bf16[128,2048]{1,0:T(8,128)(2,1)S(1)}, bf16[128,2048]{1,0:T(8,128)(2,1)S(1)}, u32[]{:S(2)}, u32[]{:S(2)}) %collective-permute-start.68) | collective-permute-done | bytes 524320 | tf_op jit(solution)/shard_map/ppermute | solution.py:197
  517.8 7.7 convert_add_fusion
  533.3 5.2 collective-permute-done.74
  553.0 5.0 collective-permute-done.78
  563.2 6.4 collective-permute-done.79
  575.7 16.4 %collective-permute-done.83 = bf16[2048,512]{1,0:T(8,128)(2,1)} collective-permute-done((bf16[2048,512]{1,0:T(8,128)(2,1)}, bf16[2048,512]{1,0:T(8,128)(2,1)}, u32[]{:S(2)}, u32[]{:S(2)}) %collective-permute-start.83) | collective-permute-done | bytes 2097184 | tf_op jit(solution)/shard_map/ppermute | solution.py:244
  592.1 5.0 add_convert_fusion.1
  601.6 10.1 %shard_map.189 = (f32[1024,512]{1,0:T(8,128)S(1)}, bf16[1024,256]{1,0:T(8,128)(2,1)S(1)}, f32[8,2,128]{2,1,0:T(2,128)S(1)}, f32[2,256]{1,0:T(2,128)S(1)}) custom-call(bf16[1024,768]{1,0:T(8,128)(2,1)S(1)} %get-tuple-element.95.rot_ref, bf16[1024,256]{1,0:T(8,128)(2,1)S(1)} %convolution_convert_fusion.4.up_ref, f32[1024,768]{1,0:T(8,128)S(1)} %copy-done.2, ...), custom_call_target="tpu_custom_call" | custom-call | flops 335544320 | bytes 7864320 | tf_op jit(solution)/shard_map/pallas_call | solution.py:645
  618.4 13.3 %collective-permute-done.110 = f32[4,2048]{1,0:T(4,128)S(1)} collective-permute-done((f32[4,2048]{1,0:T(4,128)S(1)}, f32[4,2048]{1,0:T(4,128)S(1)}, u32[]{:S(2)}, u32[]{:S(2)}) %collective-permute-start.110) | collective-permute-done | bytes 32800 | tf_op jit(solution)/shard_map/ppermute | solution.py:244
  647.6 5.1 all-to-all-start.1
  664.4 34.4 %collective-permute-done.114 = f32[4,2048]{1,0:T(4,128)S(1)} collective-permute-done((f32[4,2048]{1,0:T(4,128)S(1)}, f32[4,2048]{1,0:T(4,128)S(1)}, u32[]{:S(2)}, u32[]{:S(2)}) %collective-permute-start.114) | collective-permute-done | bytes 32800 | tf_op jit(solution)/shard_map/ppermute | solution.py:197
  710.9 5.8 collective-permute-done.92
  732.1 4.6 collective-permute-start.96
  768.3 30.8 %collective-permute-done.119.refs_2_ = bf16[8,256,512]{2,1,0:T(8,128)(2,1)S(1)} collective-permute-done((bf16[8,256,512]{2,1,0:T(8,128)(2,1)S(1)}, bf16[8,256,512]{2,1,0:T(8,128)(2,1)S(1)}, u32[]{:S(2)}, u32[]{:S(2)}) %collective-permute-start.119) | collective-permute-done | bytes 2097184 | tf_op jit(solution)/shard_map/ppermute | solution.py:244
  810.9 9.9 %collective-permute-done.116.refs_2_ = bf16[8,64,768]{2,1,0:T(8,128)(2,1)S(1)} collective-permute-done((bf16[8,64,768]{2,1,0:T(8,128)(2,1)S(1)}, bf16[8,64,768]{2,1,0:T(8,128)(2,1)S(1)}, u32[]{:S(2)}, u32[]{:S(2)}) %collective-permute-start.116) | collective-permute-done | bytes 786464 | tf_op jit(solution)/shard_map/ppermute | solution.py:244
  826.1 9.1 %shard_map.194 = f32[256,16384]{1,0:T(8,128)} custom-call(s32[1]{0:T(128)} %bitcast.36.copy_ref, bf16[8,256,512]{2,1,0:T(8,128)(2,1)S(1)} %all-to-all-done.1.refs_0_, bf16[8,256,512]{2,1,0:T(8,128)(2,1)S(1)} %collective-permute-done.118.refs_1_, bf16[8,256,512]{2,1,0:T(8,128)(2,1)S(1)} %collective-permute-done.119.refs_2_, ...), custom_call_target="tpu_custom_call" | custom-call | bytes 25165824 | tf_op jit(solution)/shard_map/pallas_call | solution.py:690
  (539 shorter events, 385.0 us)
Async XLA Ops:
  0.7 18.7 %collective-permute-start.1 = (bf16[128,2048]{1,0:T(8,128)(2,1)}, bf16[128,2048]{1,0:T(8,128)(2,1)S(1)}, u32[]{:S(2)}, u32[]{:S(2)}) collective-permute-start(bf16[128,2048]{1,0:T(8,128)(2,1)} %param.13), channel_id=1, source_target_pairs={{0,2},{1,3},{2,0},{3,1},{4,6},{5,7},{6,4},{7,5},{8,10},{9,11},{10,... | collective-permute-start | bytes 1572872 | tf_op jit(solution)/shard_map/ppermute | solution.py:197
  3.8 23.5 %collective-permute-start = (bf16[128,2048]{1,0:T(8,128)(2,1)}, bf16[128,2048]{1,0:T(8,128)(2,1)S(1)}, u32[]{:S(2)}, u32[]{:S(2)}) collective-permute-start(bf16[128,2048]{1,0:T(8,128)(2,1)} %param.13), channel_id=1, source_target_pairs={{0,1},{1,0},{2,3},{3,2},{4,5},{5,4},{6,7},{7,6},{8,9},{9,8},{10,11... | collective-permute-start | bytes 1572872 | tf_op jit(solution)/shard_map/ppermute | solution.py:197
  7.9 24.0 %collective-permute-start.6 = (bf16[64,768]{1,0:T(8,128)(2,1)}, bf16[64,768]{1,0:T(8,128)(2,1)S(1)}, u32[]{:S(2)}, u32[]{:S(2)}) collective-permute-start(bf16[64,768]{1,0:T(8,128)(2,1)} %pad_maximum_fusion.3), channel_id=1, source_target_pairs={{0,2},{1,3},{2,0},{3,1},{4,6},{5,7},{6,4},{7,5},{8,10},{9,11},{10,... | collective-permute-start | bytes 294920 | tf_op jit(solution)/shard_map/ppermute | solution.py:197
  12.9 20.4 %collective-permute-start.7 = (bf16[64,768]{1,0:T(8,128)(2,1)}, bf16[64,768]{1,0:T(8,128)(2,1)}, u32[]{:S(2)}, u32[]{:S(2)}) collective-permute-start(bf16[64,768]{1,0:T(8,128)(2,1)} %pad_maximum_fusion.4), channel_id=1, source_target_pairs={{0,3},{1,2},{2,1},{3,0},{4,7},{5,6},{6,5},{7,4},{8,11},{9,10},{10,... | collective-permute-start | bytes 294920 | tf_op jit(solution)/shard_map/ppermute | solution.py:197
  21.6 17.7 %collective-permute-start.9 = (bf16[64,768]{1,0:T(8,128)(2,1)}, bf16[64,768]{1,0:T(8,128)(2,1)S(1)}, u32[]{:S(2)}, u32[]{:S(2)}) collective-permute-start(bf16[64,768]{1,0:T(8,128)(2,1)} %pad_maximum_fusion.6), channel_id=1, source_target_pairs={{0,5},{1,4},{2,7},{3,6},{4,1},{5,0},{6,3},{7,2},{8,13},{9,12},{10,... | collective-permute-start | bytes 294920 | tf_op jit(solution)/shard_map/ppermute | solution.py:197
  41.2 18.4 %collective-permute-start.12 = (bf16[128,2048]{1,0:T(8,128)(2,1)S(1)}, bf16[128,2048]{1,0:T(8,128)(2,1)S(1)}, u32[]{:S(2)}, u32[]{:S(2)}) collective-permute-start(bf16[128,2048]{1,0:T(8,128)(2,1)S(1)} %copy-done.40), channel_id=1, source_target_pairs={{4,6},{5,7},{2,0},{3,1},{12,14},{13,15},{10,8},{11,9},{20,22},{21,... | collective-permute-start | bytes 1572872 | tf_op jit(solution)/shard_map/ppermute | solution.py:201
  44.3 30.6 %collective-permute-start.17 = (bf16[8,64,768]{2,1,0:T(8,128)(2,1)S(1)}, bf16[8,64,768]{2,1,0:T(8,128)(2,1)S(1)}, u32[]{:S(2)}, u32[]{:S(2)}) collective-permute-start(bf16[8,64,768]{2,1,0:T(8,128)(2,1)S(1)} %bitcast_dynamic-update-slice_fusion.12), channel_id=1, source_target_pairs={{0,16},{8,24},{16,0},{24,8},{1,17},{9,25},{17,1},{25,9},{2,18},{10... | collective-permute-start | bytes 2359304 | tf_op jit(solution)/shard_map/ppermute | solution.py:244
  63.9 17.9 %collective-permute-start.14 = (bf16[128,2048]{1,0:T(8,128)(2,1)}, bf16[128,2048]{1,0:T(8,128)(2,1)}, u32[]{:S(2)}, u32[]{:S(2)}) collective-permute-start(bf16[128,2048]{1,0:T(8,128)(2,1)} %collective-permute-done.4), channel_id=1, source_target_pairs={{4,6},{5,7},{2,0},{3,1},{12,14},{13,15},{10,8},{11,9},{20,22},{21,... | collective-permute-start | bytes 1572872 | tf_op jit(solution)/shard_map/ppermute | solution.py:201
  65.9 110.6 %all-to-all-start = ((bf16[8,256,512]{2,1,0:T(8,128)(2,1)}), bf16[8,256,512]{2,1,0:T(8,128)(2,1)}, u32[]{:S(2)}, u32[]{:S(2)}) async-start(bf16[8,256,512]{2,1,0:T(8,128)(2,1)} %fusion.80), calls=%async_computation | async-start | bytes 4194304 | tf_op jit(solution)/shard_map/all_to_all | solution.py:539
  74.9 31.6 %collective-permute-start.18 = (bf16[8,64,768]{2,1,0:T(8,128)(2,1)S(1)}, bf16[8,64,768]{2,1,0:T(8,128)(2,1)S(1)}, u32[]{:S(2)}, u32[]{:S(2)}) collective-permute-start(bf16[8,64,768]{2,1,0:T(8,128)(2,1)S(1)} %collective-permute-done.17), channel_id=1, source_target_pairs={{0,8},{8,0},{16,24},{24,16},{1,9},{9,1},{17,25},{25,17},{2,10},{10... | collective-permute-start | bytes 2359304 | tf_op jit(solution)/shard_map/ppermute | solution.py:240
  83.0 23.5 %collective-permute-start.15 = (bf16[128,2048]{1,0:T(8,128)(2,1)S(1)}, bf16[128,2048]{1,0:T(8,128)(2,1)S(1)}, u32[]{:S(2)}, u32[]{:S(2)}) collective-permute-start(bf16[128,2048]{1,0:T(8,128)(2,1)S(1)} %get-tuple-element.153), channel_id=1, source_target_pairs={{0,1},{1,0},{2,3},{3,2},{4,5},{5,4},{6,7},{7,6},{8,9},{9,8},{10,11... | collective-permute-start | bytes 1572872 | tf_op jit(solution)/shard_map/ppermute | solution.py:197
  160.6 19.7 %collective-permute-start.29 = (bf16[128,2048]{1,0:T(8,128)(2,1)}, bf16[128,2048]{1,0:T(8,128)(2,1)}, u32[]{:S(2)}, u32[]{:S(2)}) collective-permute-start(bf16[128,2048]{1,0:T(8,128)(2,1)} %get-tuple-element.211), channel_id=1, source_target_pairs={{6,4},{7,5},{0,2},{1,3},{14,12},{15,13},{8,10},{9,11},{22,20},{23,... | collective-permute-start | bytes 1572872 | tf_op jit(solution)/shard_map/ppermute | solution.py:201
  176.5 30.5 %collective-permute-start.37 = (bf16[2048,512]{1,0:T(8,128)(2,1)}, bf16[2048,512]{1,0:T(8,128)(2,1)}, u32[]{:S(2)}, u32[]{:S(2)}) collective-permute-start(bf16[2048,512]{1,0:T(8,128)(2,1)} %bitcast.31), channel_id=1, source_target_pairs={{0,16},{8,24},{16,0},{24,8},{1,17},{9,25},{17,1},{25,9},{2,18},{10... | collective-permute-start | bytes 6291464 | tf_op jit(solution)/shard_map/ppermute | solution.py:244
  182.8 24.2 %collective-permute-start.23 = (bf16[128,2048]{1,0:T(8,128)(2,1)S(1)}, bf16[128,2048]{1,0:T(8,128)(2,1)S(1)}, u32[]{:S(2)}, u32[]{:S(2)}) collective-permute-start(bf16[128,2048]{1,0:T(8,128)(2,1)S(1)} %slice.599), channel_id=1, source_target_pairs={{0,1},{1,0},{2,3},{3,2},{4,5},{5,4},{6,7},{7,6},{8,9},{9,8},{10,11... | collective-permute-start | bytes 1572872 | tf_op jit(solution)/shard_map/ppermute | solution.py:197
  183.3 23.8 %collective-permute-start.27 = (bf16[128,2048]{1,0:T(8,128)(2,1)S(1)}, bf16[128,2048]{1,0:T(8,128)(2,1)S(1)}, u32[]{:S(2)}, u32[]{:S(2)}) collective-permute-start(bf16[128,2048]{1,0:T(8,128)(2,1)S(1)} %copy-done.44), channel_id=1, source_target_pairs={{2,4},{3,5},{4,2},{5,3},{10,12},{11,13},{12,10},{13,11},{18,20},{1... | collective-permute-start | bytes 1572872 | tf_op jit(solution)/shard_map/ppermute | solution.py:201
  188.1 19.0 %collective-permute-start.31 = (bf16[128,2048]{1,0:T(8,128)(2,1)S(1)}, bf16[128,2048]{1,0:T(8,128)(2,1)S(1)}, u32[]{:S(2)}, u32[]{:S(2)}) collective-permute-start(bf16[128,2048]{1,0:T(8,128)(2,1)S(1)} %fusion.23), channel_id=1, source_target_pairs={{0,2},{1,3},{2,0},{3,1},{4,6},{5,7},{6,4},{7,5},{8,10},{9,11},{10,... | collective-permute-start | bytes 1572872 | tf_op jit(solution)/shard_map/ppermute | solution.py:197
  191.8 48.2 %collective-permute-start.36 = (bf16[2048,512]{1,0:T(8,128)(2,1)}, bf16[2048,512]{1,0:T(8,128)(2,1)}, u32[]{:S(2)}, u32[]{:S(2)}) collective-permute-start(bf16[2048,512]{1,0:T(8,128)(2,1)} %bitcast.31), channel_id=1, source_target_pairs={{0,8},{8,0},{16,24},{24,16},{1,9},{9,1},{17,25},{25,17},{2,10},{10... | collective-permute-start | bytes 6291464 | tf_op jit(solution)/shard_map/ppermute | solution.py:240
  207.0 32.9 %collective-permute-start.38 = (bf16[2048,512]{1,0:T(8,128)(2,1)}, bf16[2048,512]{1,0:T(8,128)(2,1)}, u32[]{:S(2)}, u32[]{:S(2)}) collective-permute-start(bf16[2048,512]{1,0:T(8,128)(2,1)} %collective-permute-done.37), channel_id=1, source_target_pairs={{0,8},{8,0},{16,24},{24,16},{1,9},{9,1},{17,25},{25,17},{2,10},{10... | collective-permute-start | bytes 6291464 | tf_op jit(solution)/shard_map/ppermute | solution.py:240
  226.6 17.7 %collective-permute-start.40 = (bf16[128,2048]{1,0:T(8,128)(2,1)}, bf16[128,2048]{1,0:T(8,128)(2,1)S(1)}, u32[]{:S(2)}, u32[]{:S(2)}) collective-permute-start(bf16[128,2048]{1,0:T(8,128)(2,1)} %collective-permute-done.39), channel_id=1, source_target_pairs={{4,6},{5,7},{2,0},{3,1},{12,14},{13,15},{10,8},{11,9},{20,22},{21,... | collective-permute-start | bytes 1572872 | tf_op jit(solution)/shard_map/ppermute | solution.py:201
  240.0 17.4 %collective-permute-start.42 = (bf16[128,2048]{1,0:T(8,128)(2,1)S(1)}, bf16[128,2048]{1,0:T(8,128)(2,1)S(1)}, u32[]{:S(2)}, u32[]{:S(2)}) collective-permute-start(bf16[128,2048]{1,0:T(8,128)(2,1)S(1)} %collective-permute-done.35), channel_id=1, source_target_pairs={{4,6},{5,7},{2,0},{3,1},{12,14},{13,15},{10,8},{11,9},{20,22},{21,... | collective-permute-start | bytes 1572872 | tf_op jit(solution)/shard_map/ppermute | solution.py:201
  288.8 18.7 %collective-permute-start.45 = (bf16[128,2048]{1,0:T(8,128)(2,1)S(1)}, bf16[128,2048]{1,0:T(8,128)(2,1)S(1)}, u32[]{:S(2)}, u32[]{:S(2)}) collective-permute-start(bf16[128,2048]{1,0:T(8,128)(2,1)S(1)} %slice.594), channel_id=1, source_target_pairs={{0,1},{1,0},{2,3},{3,2},{4,5},{5,4},{6,7},{7,6},{8,9},{9,8},{10,11... | collective-permute-start | bytes 1572872 | tf_op jit(solution)/shard_map/ppermute | solution.py:197
  332.2 18.8 %collective-permute-start.52 = (bf16[128,2048]{1,0:T(8,128)(2,1)S(1)}, bf16[128,2048]{1,0:T(8,128)(2,1)S(1)}, u32[]{:S(2)}, u32[]{:S(2)}) collective-permute-start(bf16[128,2048]{1,0:T(8,128)(2,1)S(1)} %fusion.19), channel_id=1, source_target_pairs={{0,2},{1,3},{2,0},{3,1},{4,6},{5,7},{6,4},{7,5},{8,10},{9,11},{10,... | collective-permute-start | bytes 1572872 | tf_op jit(solution)/shard_map/ppermute | solution.py:197
  427.7 54.3 %collective-permute-start.62 = (bf16[512,2048]{1,0:T(8,128)(2,1)}, bf16[512,2048]{1,0:T(8,128)(2,1)S(1)}, u32[]{:S(2)}, u32[]{:S(2)}) collective-permute-start(bf16[512,2048]{1,0:T(8,128)(2,1)} %convolution_convert_fusion.2), channel_id=1, source_target_pairs={{0,8},{8,0},{16,24},{24,16},{1,9},{9,1},{17,25},{25,17},{2,10},{10... | collective-permute-start | bytes 6291464 | tf_op jit(solution)/shard_map/ppermute | solution.py:240
  442.5 22.6 %collective-permute-start.64 = (bf16[128,2048]{1,0:T(8,128)(2,1)S(1)}, bf16[128,2048]{1,0:T(8,128)(2,1)S(1)}, u32[]{:S(2)}, u32[]{:S(2)}) collective-permute-start(bf16[128,2048]{1,0:T(8,128)(2,1)S(1)} %slice.590), channel_id=1, source_target_pairs={{0,1},{1,0},{2,3},{3,2},{4,5},{5,4},{6,7},{7,6},{8,9},{9,8},{10,11... | collective-permute-start | bytes 1572872 | tf_op jit(solution)/shard_map/ppermute | solution.py:197
  475.2 35.0 %collective-permute-start.67 = (bf16[128,2048]{1,0:T(8,128)(2,1)S(1)}, bf16[128,2048]{1,0:T(8,128)(2,1)S(1)}, u32[]{:S(2)}, u32[]{:S(2)}) collective-permute-start(bf16[128,2048]{1,0:T(8,128)(2,1)S(1)} %get-tuple-element.206), channel_id=1, source_target_pairs={{2,4},{3,5},{4,2},{5,3},{10,12},{11,13},{12,10},{13,11},{18,20},{1... | collective-permute-start | bytes 1572872 | tf_op jit(solution)/shard_map/ppermute | solution.py:201
  492.5 25.3 %collective-permute-start.72 = (bf16[2048,512]{1,0:T(8,128)(2,1)S(1)}, bf16[2048,512]{1,0:T(8,128)(2,1)}, u32[]{:S(2)}, u32[]{:S(2)}) collective-permute-start(bf16[2048,512]{1,0:T(8,128)(2,1)S(1)} %copy-done.62), channel_id=1, source_target_pairs={{0,8},{8,0},{16,24},{24,16},{1,9},{9,1},{17,25},{25,17},{2,10},{10... | collective-permute-start | bytes 6291464 | tf_op jit(solution)/shard_map/ppermute | solution.py:240
  496.3 18.3 %collective-permute-start.63 = (bf16[128,2048]{1,0:T(8,128)(2,1)S(1)}, bf16[128,2048]{1,0:T(8,128)(2,1)S(1)}, u32[]{:S(2)}, u32[]{:S(2)}) collective-permute-start(bf16[128,2048]{1,0:T(8,128)(2,1)S(1)} %slice.591), channel_id=1, source_target_pairs={{0,1},{1,0},{2,3},{3,2},{4,5},{5,4},{6,7},{7,6},{8,9},{9,8},{10,11... | collective-permute-start | bytes 1572872 | tf_op jit(solution)/shard_map/ppermute | solution.py:197
  510.2 29.3 %collective-permute-start.82 = (bf16[2048,512]{1,0:T(8,128)(2,1)S(1)}, bf16[2048,512]{1,0:T(8,128)(2,1)S(1)}, u32[]{:S(2)}, u32[]{:S(2)}) collective-permute-start(bf16[2048,512]{1,0:T(8,128)(2,1)S(1)} %convolution_convert_fusion.1), channel_id=1, source_target_pairs={{0,8},{8,0},{16,24},{24,16},{1,9},{9,1},{17,25},{25,17},{2,10},{10... | collective-permute-start | bytes 6291464 | tf_op jit(solution)/shard_map/ppermute | solution.py:240
  543.3 48.8 %collective-permute-start.83 = (bf16[2048,512]{1,0:T(8,128)(2,1)}, bf16[2048,512]{1,0:T(8,128)(2,1)}, u32[]{:S(2)}, u32[]{:S(2)}) collective-permute-start(bf16[2048,512]{1,0:T(8,128)(2,1)} %add_convert_fusion.2), channel_id=1, source_target_pairs={{0,16},{8,24},{16,0},{24,8},{1,17},{9,25},{17,1},{25,9},{2,18},{10... | collective-permute-start | bytes 6291464 | tf_op jit(solution)/shard_map/ppermute | solution.py:244
  562.7 97.8 %collective-permute-start.121 = (bf16[512,2048]{1,0:T(8,128)(2,1)}, bf16[512,2048]{1,0:T(8,128)(2,1)}, u32[]{:S(2)}, u32[]{:S(2)}) collective-permute-start(bf16[512,2048]{1,0:T(8,128)(2,1)} %add_convert_fusion.3), channel_id=1, source_target_pairs={{0,16},{8,24},{16,0},{24,8},{1,17},{9,25},{17,1},{25,9},{2,18},{10... | collective-permute-start | bytes 6291464 | tf_op jit(solution)/shard_map/ppermute | solution.py:244
  574.9 22.2 %collective-permute-start.81 = (bf16[128,2048]{1,0:T(8,128)(2,1)S(1)}, bf16[128,2048]{1,0:T(8,128)(2,1)S(1)}, u32[]{:S(2)}, u32[]{:S(2)}) collective-permute-start(bf16[128,2048]{1,0:T(8,128)(2,1)S(1)} %get-tuple-element.131), channel_id=1, source_target_pairs={{0,1},{1,0},{2,3},{3,2},{4,5},{5,4},{6,7},{7,6},{8,9},{9,8},{10,11... | collective-permute-start | bytes 1572872 | tf_op jit(solution)/shard_map/ppermute | solution.py:197
  613.0 18.6 %collective-permute-start.110 = (f32[4,2048]{1,0:T(4,128)S(1)}, f32[4,2048]{1,0:T(4,128)S(1)}, u32[]{:S(2)}, u32[]{:S(2)}) collective-permute-start(f32[4,2048]{1,0:T(4,128)S(1)} %pad_maximum_fusion.10), channel_id=1, source_target_pairs={{0,16},{8,24},{16,0},{24,8},{1,17},{9,25},{17,1},{25,9},{2,18},{10... | collective-permute-start | bytes 98312 | tf_op jit(solution)/shard_map/ppermute | solution.py:244
  618.4 37.4 %collective-permute-start.88 = (bf16[128,2048]{1,0:T(8,128)(2,1)}, bf16[128,2048]{1,0:T(8,128)(2,1)}, u32[]{:S(2)}, u32[]{:S(2)}) collective-permute-start(bf16[128,2048]{1,0:T(8,128)(2,1)} %convolution_convert_fusion.3), channel_id=1, source_target_pairs={{0,8},{8,0},{16,24},{24,16},{1,9},{9,1},{17,25},{25,17},{2,10},{10... | collective-permute-start | bytes 1572872 | tf_op jit(solution)/shard_map/ppermute | solution.py:240
  647.6 109.0 %all-to-all-start.1 = ((bf16[8,256,512]{2,1,0:T(8,128)(2,1)}), bf16[8,256,512]{2,1,0:T(8,128)(2,1)S(1)}, u32[]{:S(2)}, u32[]{:S(2)}) async-start(bf16[8,256,512]{2,1,0:T(8,128)(2,1)} %bitcast.180), calls=%async_computation.1 | async-start | bytes 4194304 | tf_op jit(solution)/shard_map/all_to_all | solution.py:630
  652.7 46.0 %collective-permute-start.114 = (f32[4,2048]{1,0:T(4,128)S(1)}, f32[4,2048]{1,0:T(4,128)S(1)}, u32[]{:S(2)}, u32[]{:S(2)}) collective-permute-start(f32[4,2048]{1,0:T(4,128)S(1)} %add.765), channel_id=1, source_target_pairs={{0,4},{1,5},{2,6},{3,7},{4,0},{5,1},{6,2},{7,3},{8,12},{9,13},{10,... | collective-permute-start | bytes 98312 | tf_op jit(solution)/shard_map/ppermute | solution.py:197
  658.9 39.9 %collective-permute-start.89 = (bf16[128,2048]{1,0:T(8,128)(2,1)S(1)}, bf16[128,2048]{1,0:T(8,128)(2,1)S(1)}, u32[]{:S(2)}, u32[]{:S(2)}) collective-permute-start(bf16[128,2048]{1,0:T(8,128)(2,1)S(1)} %fusion), channel_id=1, source_target_pairs={{0,16},{8,24},{16,0},{24,8},{1,17},{9,25},{17,1},{25,9},{2,18},{10... | collective-permute-start | bytes 1572872 | tf_op jit(solution)/shard_map/ppermute | solution.py:244
  663.0 80.9 %collective-permute-start.122 = (bf16[512,2048]{1,0:T(8,128)(2,1)S(1)}, bf16[512,2048]{1,0:T(8,128)(2,1)S(1)}, u32[]{:S(2)}, u32[]{:S(2)}) collective-permute-start(bf16[512,2048]{1,0:T(8,128)(2,1)S(1)} %add_convert_fusion), channel_id=1, source_target_pairs={{0,8},{8,0},{16,24},{24,16},{1,9},{9,1},{17,25},{25,17},{2,10},{10... | collective-permute-start | bytes 6291464 | tf_op jit(solution)/shard_map/ppermute | solution.py:240
  708.5 28.2 %collective-permute-start.99 = (bf16[8,64,768]{2,1,0:T(8,128)(2,1)S(1)}, bf16[8,64,768]{2,1,0:T(8,128)(2,1)S(1)}, u32[]{:S(2)}, u32[]{:S(2)}) collective-permute-start(bf16[8,64,768]{2,1,0:T(8,128)(2,1)S(1)} %get-tuple-element.108), channel_id=1, source_target_pairs={{0,8},{8,0},{16,24},{24,16},{1,9},{9,1},{17,25},{25,17},{2,10},{10... | collective-permute-start | bytes 2359304 | tf_op jit(solution)/shard_map/ppermute | solution.py:240
  721.2 18.1 %collective-permute-start.101 = (bf16[8,64,768]{2,1,0:T(8,128)(2,1)S(1)}, bf16[8,64,768]{2,1,0:T(8,128)(2,1)S(1)}, u32[]{:S(2)}, u32[]{:S(2)}) collective-permute-start(bf16[8,64,768]{2,1,0:T(8,128)(2,1)S(1)} %fusion.1), channel_id=1, source_target_pairs={{0,16},{8,24},{16,0},{24,8},{1,17},{9,25},{17,1},{25,9},{2,18},{10... | collective-permute-start | bytes 2359304 | tf_op jit(solution)/shard_map/ppermute | solution.py:244
  732.1 18.2 %collective-permute-start.96 = (bf16[128,2048]{1,0:T(8,128)(2,1)S(1)}, bf16[128,2048]{1,0:T(8,128)(2,1)S(1)}, u32[]{:S(2)}, u32[]{:S(2)}) collective-permute-start(bf16[128,2048]{1,0:T(8,128)(2,1)S(1)} %get-tuple-element.205), channel_id=1, source_target_pairs={{6,4},{7,5},{0,2},{1,3},{14,12},{15,13},{8,10},{9,11},{22,20},{23,... | collective-permute-start | bytes 1572872 | tf_op jit(solution)/shard_map/ppermute | solution.py:201
  756.6 42.5 %collective-permute-start.119 = (bf16[8,256,512]{2,1,0:T(8,128)(2,1)S(1)}, bf16[8,256,512]{2,1,0:T(8,128)(2,1)S(1)}, u32[]{:S(2)}, u32[]{:S(2)}) collective-permute-start(bf16[8,256,512]{2,1,0:T(8,128)(2,1)S(1)} %all-to-all-done.1.refs_0_), channel_id=1, source_target_pairs={{0,16},{8,24},{16,0},{24,8},{1,17},{9,25},{17,1},{25,9},{2,18},{10... | collective-permute-start | bytes 6291464 | tf_op jit(solution)/shard_map/ppermute | solution.py:244
  760.0 40.0 %collective-permute-start.95 = (bf16[128,2048]{1,0:T(8,128)(2,1)}, bf16[128,2048]{1,0:T(8,128)(2,1)S(1)}, u32[]{:S(2)}, u32[]{:S(2)}) collective-permute-start(bf16[128,2048]{1,0:T(8,128)(2,1)} %slice.584), channel_id=1, source_target_pairs={{0,1},{1,0},{2,3},{3,2},{4,5},{5,4},{6,7},{7,6},{8,9},{9,8},{10,11... | collective-permute-start | bytes 1572872 | tf_op jit(solution)/shard_map/ppermute | solution.py:197
  761.4 42.3 %collective-permute-start.90 = (bf16[128,2048]{1,0:T(8,128)(2,1)}, bf16[128,2048]{1,0:T(8,128)(2,1)S(1)}, u32[]{:S(2)}, u32[]{:S(2)}) collective-permute-start(bf16[128,2048]{1,0:T(8,128)(2,1)} %slice.587), channel_id=1, source_target_pairs={{0,1},{1,0},{2,3},{3,2},{4,5},{5,4},{6,7},{7,6},{8,9},{9,8},{10,11... | collective-permute-start | bytes 1572872 | tf_op jit(solution)/shard_map/ppermute | solution.py:197
  762.1 38.7 %collective-permute-start.97 = (bf16[128,2048]{1,0:T(8,128)(2,1)S(1)}, bf16[128,2048]{1,0:T(8,128)(2,1)S(1)}, u32[]{:S(2)}, u32[]{:S(2)}) collective-permute-start(bf16[128,2048]{1,0:T(8,128)(2,1)S(1)} %add_convert_fusion.5), channel_id=1, source_target_pairs={{2,4},{3,5},{4,2},{5,3},{10,12},{11,13},{12,10},{13,11},{18,20},{1... | collective-permute-start | bytes 1572872 | tf_op jit(solution)/shard_map/ppermute | solution.py:201
  768.3 57.9 %collective-permute-start.118 = (bf16[8,256,512]{2,1,0:T(8,128)(2,1)S(1)}, bf16[8,256,512]{2,1,0:T(8,128)(2,1)S(1)}, u32[]{:S(2)}, u32[]{:S(2)}) collective-permute-start(bf16[8,256,512]{2,1,0:T(8,128)(2,1)S(1)} %all-to-all-done.1.refs_0_), channel_id=1, source_target_pairs={{0,8},{8,0},{16,24},{24,16},{1,9},{9,1},{17,25},{25,17},{2,10},{10... | collective-permute-start | bytes 6291464 | tf_op jit(solution)/shard_map/ppermute | solution.py:240
  799.1 27.0 %collective-permute-start.120 = (bf16[8,256,512]{2,1,0:T(8,128)(2,1)S(1)}, bf16[8,256,512]{2,1,0:T(8,128)(2,1)S(1)}, u32[]{:S(2)}, u32[]{:S(2)}) collective-permute-start(bf16[8,256,512]{2,1,0:T(8,128)(2,1)S(1)} %collective-permute-done.119.refs_2_), channel_id=1, source_target_pairs={{0,8},{8,0},{16,24},{24,16},{1,9},{9,1},{17,25},{25,17},{2,10},{10... | collective-permute-start | bytes 6291464 | tf_op jit(solution)/shard_map/ppermute | solution.py:240
  800.7 20.0 %collective-permute-start.116 = (bf16[8,64,768]{2,1,0:T(8,128)(2,1)S(1)}, bf16[8,64,768]{2,1,0:T(8,128)(2,1)S(1)}, u32[]{:S(2)}, u32[]{:S(2)}) collective-permute-start(bf16[8,64,768]{2,1,0:T(8,128)(2,1)S(1)} %bitcast_dynamic-update-slice_fusion.4.refs_0_), channel_id=1, source_target_pairs={{0,16},{8,24},{16,0},{24,8},{1,17},{9,25},{17,1},{25,9},{2,18},{10... | collective-permute-start | bytes 2359304 | tf_op jit(solution)/shard_map/ppermute | solution.py:244
  803.7 17.7 %collective-permute-start.98 = (bf16[128,2048]{1,0:T(8,128)(2,1)S(1)}, bf16[128,2048]{1,0:T(8,128)(2,1)S(1)}, u32[]{:S(2)}, u32[]{:S(2)}) collective-permute-start(bf16[128,2048]{1,0:T(8,128)(2,1)S(1)} %fusion.5), channel_id=1, source_target_pairs={{0,2},{1,3},{2,0},{3,1},{4,6},{5,7},{6,4},{7,5},{8,10},{9,11},{10,... | collective-permute-start | bytes 1572872 | tf_op jit(solution)/shard_map/ppermute | solution.py:197
  (144 other events, 2316.4 us)
